TPU v7x, 32 devices: a whole 2x2x4 slice. The times are simulated.
32 devices in a mesh: dp: 2 (over x), fsdp: 16 (over z, y, core).
Axes of the slice: x: 2, y: 2, z: 4, core: 2. Of those that a mesh axis runs over, the one named last changes fastest.
Arguments:
- text_a: bfloat16 [32, 48, 768], P(('dp', 'fsdp')), may hold values from -6 to 6
- visual_a: bfloat16 [32, 20, 768], P(('dp', 'fsdp')), may hold values from -6 to 6
- text_b: bfloat16 [32, 56, 768], P(('dp', 'fsdp')), may hold values from -6 to 6
- visual_b: bfloat16 [32, 28, 768], P(('dp', 'fsdp')), may hold values from -6 to 6
- text_len_a: int32 [32], P(('dp', 'fsdp')), may hold values from 24 to 48
- visual_len_a: int32 [32], P(('dp', 'fsdp')), may hold values from 10 to 20
- text_len_b: int32 [32], P(('dp', 'fsdp')), may hold values from 28 to 56
- visual_len_b: int32 [32], P(('dp', 'fsdp')), may hold values from 14 to 28
- cot_text_a: bfloat16 [32, 48, 768], P(('dp', 'fsdp')), may hold values from -6 to 6
- cot_visual_a: bfloat16 [32, 20, 768], P(('dp', 'fsdp')), may hold values from -6 to 6
- cot_text_b: bfloat16 [32, 56, 768], P(('dp', 'fsdp')), may hold values from -6 to 6
- cot_visual_b: bfloat16 [32, 28, 768], P(('dp', 'fsdp')), may hold values from -6 to 6
- attn_in: bfloat16 [2, 6, 768, 768], P(None, None, 'fsdp'), may hold values from -0.21875 to 0.21875
- attn_out: bfloat16 [2, 2, 768, 768], P(None, None, 'fsdp'), may hold values from -0.625 to 0.625
- ffn_up: bfloat16 [2, 768, 3072], P(None, 'fsdp'), may hold values from -0.21875 to 0.21875
- ffn_down: bfloat16 [2, 3072, 768], P(None, 'fsdp'), may hold values from -0.109375 to 0.109375
- norm_gain: bfloat16 [2, 3, 768], P(None, None, 'fsdp'), may hold values from 0.5 to 1.5
- norm_bias: bfloat16 [2, 3, 768], P(None, None, 'fsdp'), may hold values from -2 to 2
- gate_vector: bfloat16 [2, 768], P(None, 'fsdp'), may hold values from -0.21875 to 0.21875
Outputs:
- out_text_a: bfloat16 [32, 48, 768], P(('dp', 'fsdp'))
- out_visual_a: bfloat16 [32, 20, 768], P(('dp', 'fsdp'))
- out_text_b: bfloat16 [32, 56, 768], P(('dp', 'fsdp'))
- out_visual_b: bfloat16 [32, 28, 768], P(('dp', 'fsdp'))
- grad_text_a: bfloat16 [32, 48, 768], P(('dp', 'fsdp'))
- grad_visual_a: bfloat16 [32, 20, 768], P(('dp', 'fsdp'))
- grad_text_b: bfloat16 [32, 56, 768], P(('dp', 'fsdp'))
- grad_visual_b: bfloat16 [32, 28, 768], P(('dp', 'fsdp'))
- grad_attn_in: float32 [2, 6, 768, 768], P(None, None, 'fsdp')
- grad_attn_out: float32 [2, 2, 768, 768], P(None, None, 'fsdp')
- grad_ffn_up: float32 [2, 768, 3072], P(None, 'fsdp')
- grad_ffn_down: float32 [2, 3072, 768], P(None, 'fsdp')
- grad_norm_gain: float32 [2, 3, 768], P(None, None, 'fsdp')
- grad_norm_bias: float32 [2, 3, 768], P(None, None, 'fsdp')
- grad_gate_vector: float32 [2, 768], P(None, 'fsdp')
All inputs are finite; a program needn't handle non-finite values.
Results may differ from a plain program's by a relative error of at most 0.019.
Values may be sent and summed in bfloat16 or wider, within the bound.
A program may use at most 320 MiB of HBM per device.

v0:
```python
from functools import partial
import math

import jax
import jax.numpy as jnp
from jax import lax
from jax.sharding import PartitionSpec as P

HEADS = 12


def project(rows, matrix):
    return jnp.einsum("pld,de->ple", rows, matrix, preferred_element_type=jnp.float32)


def project_back(grads, matrix):
    return jnp.einsum("ple,de->pld", grads, matrix, preferred_element_type=jnp.float32)


def weight_grad(rows, grads):
    return jnp.einsum("pld,ple->de", rows, grads, preferred_element_type=jnp.float32)


def layer_norm(resid, gain_row, bias_row):
    centre = resid - jnp.mean(resid, axis=-1, keepdims=True)
    spread = jnp.mean(centre * centre, axis=-1, keepdims=True)
    return centre * lax.rsqrt(spread + 1e-05) * gain_row + bias_row


def gate_tail(resid, gain_row, bias_row, gate_row, row_mask):
    hidden_three = layer_norm(resid, gain_row, bias_row)
    logit = jnp.einsum("pld,d->pl", hidden_three, gate_row, precision=lax.Precision.HIGHEST)
    return hidden_three * (jax.nn.sigmoid(logit) * row_mask)[..., None]


def exact_gelu(upward):
    return jax.nn.gelu(upward, approximate=False)


def split_heads(rows):
    return rows.reshape(rows.shape[0], rows.shape[1], HEADS, rows.shape[2] // HEADS)


def masked_scores(queries, key_rows, key_mask):
    score_scale = 1.0 / math.sqrt(queries.shape[2] // HEADS)
    scores = (
        jnp.einsum(
            "plhe,pmhe->phlm",
            split_heads(queries),
            split_heads(key_rows),
            preferred_element_type=jnp.float32,
        )
        * score_scale
    )
    return jnp.where(key_mask[:, None, None, :], scores, -1000000000.0)


def attend_forward(queries, key_rows, value_rows, key_mask):
    masked = masked_scores(queries, key_rows, key_mask)
    row_max = jnp.max(masked, axis=-1, keepdims=True)
    expon = jnp.exp(masked - row_max)
    row_sum = jnp.sum(expon, axis=-1, keepdims=True)
    probs = expon / row_sum
    log_total = row_max + jnp.log(row_sum)
    mixed = jnp.einsum(
        "phlm,pmhe->plhe",
        probs.astype(jnp.bfloat16),
        split_heads(value_rows),
        preferred_element_type=jnp.float32,
    )
    return (mixed.reshape(queries.shape).astype(jnp.bfloat16), log_total)


def attend_backward(queries, key_rows, value_rows, key_mask, log_total, grad_mixed):
    score_scale = 1.0 / math.sqrt(queries.shape[2] // HEADS)
    masked = masked_scores(queries, key_rows, key_mask)
    probs = jnp.where(key_mask[:, None, None, :], jnp.exp(masked - log_total), 0.0)
    grad_heads = split_heads(grad_mixed)
    grad_probs = jnp.einsum(
        "plhe,pmhe->phlm", grad_heads, split_heads(value_rows), preferred_element_type=jnp.float32
    )
    grad_scores = (
        probs * (grad_probs - jnp.sum(grad_probs * probs, axis=-1, keepdims=True))
    ).astype(jnp.bfloat16)
    grad_query = (
        jnp.einsum(
            "phlm,pmhe->plhe",
            grad_scores,
            split_heads(key_rows),
            preferred_element_type=jnp.float32,
        )
        * score_scale
    )
    grad_key = (
        jnp.einsum(
            "phlm,plhe->pmhe", grad_scores, split_heads(queries), preferred_element_type=jnp.float32
        )
        * score_scale
    )
    grad_value = jnp.einsum(
        "phlm,plhe->pmhe",
        probs.astype(jnp.bfloat16),
        grad_heads,
        preferred_element_type=jnp.float32,
    )
    return (
        grad_query.reshape(queries.shape).astype(jnp.bfloat16),
        grad_key.reshape(key_rows.shape).astype(jnp.bfloat16),
        grad_value.reshape(value_rows.shape).astype(jnp.bfloat16),
    )


def cross_forward(own_rows, other_rows, other_keys, attn_in):
    cross_query = project(own_rows, attn_in[0]).astype(jnp.bfloat16)
    cross_key = project(other_rows, attn_in[1]).astype(jnp.bfloat16)
    cross_value = project(other_rows, attn_in[2]).astype(jnp.bfloat16)
    cross_mixed, cross_total = attend_forward(cross_query, cross_key, cross_value, other_keys)
    return ((cross_query, cross_key, cross_value), cross_mixed, cross_total)


def stream_forward(own_rows, other_rows, own_keys, other_keys, row_mask, params):
    attn_in, attn_out, ffn_up, ffn_down, gains, biases, gate_row = params
    _, cross_mixed, _ = cross_forward(own_rows, other_rows, other_keys, attn_in)
    resid_one = own_rows.astype(jnp.float32) + project(cross_mixed, attn_out[0])
    hidden_one = layer_norm(resid_one, gains[0], biases[0])
    hidden_low = hidden_one.astype(jnp.bfloat16)
    self_query = project(hidden_low, attn_in[3]).astype(jnp.bfloat16)
    self_key = project(hidden_low, attn_in[4]).astype(jnp.bfloat16)
    self_value = project(hidden_low, attn_in[5]).astype(jnp.bfloat16)
    self_mixed, self_total = attend_forward(self_query, self_key, self_value, own_keys)
    resid_two = hidden_one + project(self_mixed, attn_out[1])
    hidden_two = layer_norm(resid_two, gains[1], biases[1])
    ffn_in = hidden_two.astype(jnp.bfloat16)
    upward = project(ffn_in, ffn_up)
    active = exact_gelu(upward).astype(jnp.bfloat16)
    resid_three = hidden_two + project(active, ffn_down)
    output = gate_tail(resid_three, gains[2], biases[2], gate_row, row_mask)
    saved_rows = (
        resid_one,
        hidden_low,
        self_query,
        self_key,
        self_value,
        self_total,
        self_mixed,
        resid_two,
        ffn_in,
        upward,
        active,
        resid_three,
    )
    return (output, saved_rows)


def stream_backward(
    own_rows, other_rows, own_keys, other_keys, row_mask, params, saved_rows, grad_out
):
    attn_in, attn_out, ffn_up, ffn_down, gains, biases, gate_row = params
    (
        resid_one,
        hidden_low,
        self_query,
        self_key,
        self_value,
        self_total,
        self_mixed,
        resid_two,
        ffn_in,
        upward,
        active,
        resid_three,
    ) = saved_rows
    _, tail_pull = jax.vjp(
        partial(gate_tail, row_mask=row_mask), resid_three, gains[2], biases[2], gate_row
    )
    grad_three, gain_three, bias_three, grad_gate = tail_pull(grad_out)
    grad_down_in = grad_three.astype(jnp.bfloat16)
    down_grad = weight_grad(active, grad_down_in)
    grad_active = project_back(grad_down_in, ffn_down)
    _, gelu_pull = jax.vjp(exact_gelu, upward)
    grad_upward = gelu_pull(grad_active)[0].astype(jnp.bfloat16)
    up_grad = weight_grad(ffn_in, grad_upward)
    grad_two = grad_three + project_back(grad_upward, ffn_up)
    _, norm_two_pull = jax.vjp(layer_norm, resid_two, gains[1], biases[1])
    grad_resid_two, gain_two, bias_two = norm_two_pull(grad_two)
    grad_self_out = grad_resid_two.astype(jnp.bfloat16)
    self_out_grad = weight_grad(self_mixed, grad_self_out)
    grad_self_mixed = project_back(grad_self_out, attn_out[1]).astype(jnp.bfloat16)
    grad_self_query, grad_self_key, grad_self_value = attend_backward(
        self_query, self_key, self_value, own_keys, self_total, grad_self_mixed
    )
    grad_one = (
        grad_resid_two
        + project_back(grad_self_query, attn_in[3])
        + project_back(grad_self_key, attn_in[4])
        + project_back(grad_self_value, attn_in[5])
    )
    _, norm_one_pull = jax.vjp(layer_norm, resid_one, gains[0], biases[0])
    grad_resid_one, gain_one, bias_one = norm_one_pull(grad_one)
    grad_cross_out = grad_resid_one.astype(jnp.bfloat16)
    (cross_query, cross_key, cross_value), cross_mixed, cross_total = cross_forward(
        own_rows, other_rows, other_keys, attn_in
    )
    cross_out_grad = weight_grad(cross_mixed, grad_cross_out)
    grad_cross_mixed = project_back(grad_cross_out, attn_out[0]).astype(jnp.bfloat16)
    grad_cross_query, grad_cross_key, grad_cross_value = attend_backward(
        cross_query, cross_key, cross_value, other_keys, cross_total, grad_cross_mixed
    )
    grad_own = grad_resid_one + project_back(grad_cross_query, attn_in[0])
    grad_other = project_back(grad_cross_key, attn_in[1]) + project_back(
        grad_cross_value, attn_in[2]
    )
    in_grads = jnp.stack(
        [
            weight_grad(own_rows, grad_cross_query),
            weight_grad(other_rows, grad_cross_key),
            weight_grad(other_rows, grad_cross_value),
            weight_grad(hidden_low, grad_self_query),
            weight_grad(hidden_low, grad_self_key),
            weight_grad(hidden_low, grad_self_value),
        ]
    )
    out_grads = jnp.stack([cross_out_grad, self_out_grad])
    gain_grads = jnp.stack([gain_one, gain_two, gain_three])
    bias_grads = jnp.stack([bias_one, bias_two, bias_three])
    return (
        grad_own,
        grad_other,
        (in_grads, out_grads, up_grad, down_grad, gain_grads, bias_grads, grad_gate),
    )


def stream_params(gathered, stream):
    return (
        gathered[0][stream],
        gathered[1][stream],
        gathered[2][stream],
        gathered[3][stream],
        gathered[4][stream].astype(jnp.float32),
        gathered[5][stream].astype(jnp.float32),
        gathered[6][stream].astype(jnp.float32),
    )


def per_device(
    text_a,
    visual_a,
    text_b,
    visual_b,
    text_len_a,
    visual_len_a,
    text_len_b,
    visual_len_b,
    cot_text_a,
    cot_visual_a,
    cot_text_b,
    cot_visual_b,
    attn_in,
    attn_out,
    ffn_up,
    ffn_down,
    norm_gain,
    norm_bias,
    gate_vector,
):
    gathered = (
        lax.all_gather(attn_in, "fsdp", axis=2, tiled=True),
        lax.all_gather(attn_out, "fsdp", axis=2, tiled=True),
        lax.all_gather(ffn_up, "fsdp", axis=1, tiled=True),
        lax.all_gather(ffn_down, "fsdp", axis=1, tiled=True),
        lax.all_gather(norm_gain, "fsdp", axis=2, tiled=True),
        lax.all_gather(norm_bias, "fsdp", axis=2, tiled=True),
        lax.all_gather(gate_vector, "fsdp", axis=1, tiled=True),
    )
    layouts = []
    for rows_text, rows_visual, len_text, len_visual, cot_text, cot_visual in (
        (text_a, visual_a, text_len_a, visual_len_a, cot_text_a, cot_visual_a),
        (text_b, visual_b, text_len_b, visual_len_b, cot_text_b, cot_visual_b),
    ):
        keys_text = jnp.arange(rows_text.shape[1], dtype=jnp.int32)[None, :] < len_text[:, None]
        keys_visual = (
            jnp.arange(rows_visual.shape[1], dtype=jnp.int32)[None, :] < len_visual[:, None]
        )
        stream_rows = (rows_text, rows_visual)
        stream_keys = (keys_text, keys_visual)
        stream_masks = (keys_text.astype(jnp.float32), keys_visual.astype(jnp.float32))
        outputs = []
        saved_list = []
        for stream in (0, 1):
            other_side = 1 - stream
            output, saved_rows = stream_forward(
                stream_rows[stream],
                stream_rows[other_side],
                stream_keys[stream],
                stream_keys[other_side],
                stream_masks[stream],
                stream_params(gathered, stream),
            )
            outputs.append(output.astype(jnp.bfloat16))
            saved_list.append(saved_rows)
        layouts.append(
            (stream_rows, stream_keys, stream_masks, (cot_text, cot_visual), outputs, saved_list)
        )
    back_weights = (
        lax.all_gather(attn_in, "fsdp", axis=2, tiled=True),
        lax.all_gather(attn_out, "fsdp", axis=2, tiled=True),
        lax.all_gather(ffn_up, "fsdp", axis=1, tiled=True),
        lax.all_gather(ffn_down, "fsdp", axis=1, tiled=True),
        lax.all_gather(norm_gain, "fsdp", axis=2, tiled=True),
        lax.all_gather(norm_bias, "fsdp", axis=2, tiled=True),
        lax.all_gather(gate_vector, "fsdp", axis=1, tiled=True),
    )
    input_grads = [[None, None], [None, None]]
    stream_grads = []
    for stream in (0, 1):
        other_side = 1 - stream
        params = stream_params(back_weights, stream)
        summed = None
        for layout_index in (0, 1):
            stream_rows, stream_keys, stream_masks, cotangents, outputs, saved_list = layouts[
                layout_index
            ]
            grad_own, grad_other, grads_here = stream_backward(
                stream_rows[stream],
                stream_rows[other_side],
                stream_keys[stream],
                stream_keys[other_side],
                stream_masks[stream],
                params,
                saved_list[stream],
                cotangents[stream].astype(jnp.float32),
            )
            for target, piece in ((stream, grad_own), (other_side, grad_other)):
                if input_grads[layout_index][target] is None:
                    input_grads[layout_index][target] = piece
                else:
                    input_grads[layout_index][target] = input_grads[layout_index][target] + piece
            if summed is None:
                summed = grads_here
            else:
                summed = tuple((left + right for left, right in zip(summed, grads_here)))
        stream_grads.append(summed)
    text_grads = stream_grads[0]
    visual_grads = stream_grads[1]
    row_dims = (1, 1, 0, 0, 1, 1, 0)
    packed = tuple(
        (
            jnp.concatenate([text_grads[index], visual_grads[index]], axis=row_dims[index])
            for index in range(7)
        )
    )
    shares = (
        lax.psum_scatter(packed[0], ("dp", "fsdp"), scatter_dimension=1, tiled=True),
        lax.psum_scatter(packed[1], ("dp", "fsdp"), scatter_dimension=1, tiled=True),
        lax.psum_scatter(packed[2], ("dp", "fsdp"), scatter_dimension=0, tiled=True),
        lax.psum_scatter(packed[3], ("dp", "fsdp"), scatter_dimension=0, tiled=True),
        lax.psum_scatter(packed[4], ("dp", "fsdp"), scatter_dimension=1, tiled=True),
        lax.psum_scatter(packed[5], ("dp", "fsdp"), scatter_dimension=1, tiled=True),
        lax.psum_scatter(packed[6], ("dp", "fsdp"), scatter_dimension=0, tiled=True),
    )
    joined = (
        lax.all_gather(shares[0].astype(jnp.bfloat16), "dp", axis=1, tiled=True).astype(
            jnp.float32
        ),
        lax.all_gather(shares[1].astype(jnp.bfloat16), "dp", axis=1, tiled=True).astype(
            jnp.float32
        ),
        lax.all_gather(shares[2].astype(jnp.bfloat16), "dp", axis=0, tiled=True).astype(
            jnp.float32
        ),
        lax.all_gather(shares[3].astype(jnp.bfloat16), "dp", axis=0, tiled=True).astype(
            jnp.float32
        ),
        lax.all_gather(shares[4].astype(jnp.bfloat16), "dp", axis=1, tiled=True).astype(
            jnp.float32
        ),
        lax.all_gather(shares[5].astype(jnp.bfloat16), "dp", axis=1, tiled=True).astype(
            jnp.float32
        ),
        lax.all_gather(shares[6].astype(jnp.bfloat16), "dp", axis=0, tiled=True).astype(
            jnp.float32
        ),
    )
    finals = tuple(
        (jnp.stack(jnp.split(joined[index], 2, axis=row_dims[index])) for index in range(7))
    )
    first_outputs = layouts[0][4]
    second_outputs = layouts[1][4]
    return (
        first_outputs[0],
        first_outputs[1],
        second_outputs[0],
        second_outputs[1],
        input_grads[0][0].astype(jnp.bfloat16),
        input_grads[0][1].astype(jnp.bfloat16),
        input_grads[1][0].astype(jnp.bfloat16),
        input_grads[1][1].astype(jnp.bfloat16),
        finals[0],
        finals[1],
        finals[2],
        finals[3],
        finals[4],
        finals[5],
        finals[6],
    )


def solution(mesh):
    in_specs = (
        P(("dp", "fsdp"), None, None),
        P(("dp", "fsdp"), None, None),
        P(("dp", "fsdp"), None, None),
        P(("dp", "fsdp"), None, None),
        P(("dp", "fsdp")),
        P(("dp", "fsdp")),
        P(("dp", "fsdp")),
        P(("dp", "fsdp")),
        P(("dp", "fsdp"), None, None),
        P(("dp", "fsdp"), None, None),
        P(("dp", "fsdp"), None, None),
        P(("dp", "fsdp"), None, None),
        P(None, None, "fsdp", None),
        P(None, None, "fsdp", None),
        P(None, "fsdp", None),
        P(None, "fsdp", None),
        P(None, None, "fsdp"),
        P(None, None, "fsdp"),
        P(None, "fsdp"),
    )
    out_specs = (
        P(("dp", "fsdp"), None, None),
        P(("dp", "fsdp"), None, None),
        P(("dp", "fsdp"), None, None),
        P(("dp", "fsdp"), None, None),
        P(("dp", "fsdp"), None, None),
        P(("dp", "fsdp"), None, None),
        P(("dp", "fsdp"), None, None),
        P(("dp", "fsdp"), None, None),
        P(None, None, "fsdp", None),
        P(None, None, "fsdp", None),
        P(None, "fsdp", None),
        P(None, "fsdp", None),
        P(None, None, "fsdp"),
        P(None, None, "fsdp"),
        P(None, "fsdp"),
    )
    return jax.shard_map(
        per_device, mesh=mesh, in_specs=in_specs, out_specs=out_specs, check_vma=False
    )
```

profile of v0, /device:TPU:31, one launch (start us, length us, event | category | flops | bytes accessed | tf_op | source)
XLA Modules:
  0.0 1628.6 jit_solution(4821917124059183126)
XLA Ops:
  12.6 17.3 %all-gather = bf16[16,48,2]{1,2,0:T(2,128)(2,1)S(1)} all-gather(bf16[1,48,2]{1,2,0:T(2,128)(2,1)} %bitcast.1046), channel_id=1, replica_groups=mesh['dp'=2,'fsdp'=16] {'fsdp'}, dimensions={0}, use_global_device_ids=true | all-gather | bytes 3264 | tf_op jit(solution)/shard_map/all_gather | solution.py:273
  31.7 22.3 %all_gather.52 = bf16[2,3,768]{1,0,2:T(2,128)(2,1)S(1)} all-gather(bf16[2,3,48]{1,0,2:T(2,128)(2,1)S(1)} %copy.440), channel_id=1, replica_groups=mesh['dp'=2,'fsdp'=16] {'fsdp'}, dimensions={2}, use_global_device_ids=true | all-gather | bytes 9792 | tf_op jit(solution)/shard_map/all_gather | solution.py:272
  54.0 22.4 %all_gather.51 = bf16[2,3,768]{1,0,2:T(2,128)(2,1)S(1)} all-gather(bf16[2,3,48]{1,0,2:T(2,128)(2,1)S(1)} %copy.439), channel_id=1, replica_groups=mesh['dp'=2,'fsdp'=16] {'fsdp'}, dimensions={2}, use_global_device_ids=true | all-gather | bytes 9792 | tf_op jit(solution)/shard_map/all_gather | solution.py:271
  79.8 12.6 slice_reduce_fusion.1
  92.3 12.9 slice_reduce_fusion
  105.2 18.8 %all-gather.8.cloned.1.call-done = bf16[2,6,768,768]{3,2,1,0:T(8,128)(2,1)} async-done(((bf16[2,6,48,768]{3,2,1,0:T(8,128)(2,1)}), bf16[2,6,768,768]{3,2,1,0:T(8,128)(2,1)}) %all-gather.8.cloned.1.call-update) | async-done | bytes 14155792 | tf_op jit(solution)/shard_map/all_gather | solution.py:267
  131.8 46.5 %all-gather.10.cloned.1.call-done = bf16[2,2,768,768]{3,2,1,0:T(8,128)(2,1)} async-done(((bf16[2,2,48,768]{3,2,1,0:T(8,128)(2,1)}), bf16[2,2,768,768]{3,2,1,0:T(8,128)(2,1)}) %all-gather.10.cloned.1.call-update) | async-done | bytes 4718608 | tf_op jit(solution)/shard_map/all_gather | solution.py:268
  188.6 71.4 %all-gather.12.cloned.1.call-done = bf16[2,768,3072]{2,1,0:T(8,128)(2,1)} async-done(((bf16[2,48,3072]{2,1,0:T(8,128)(2,1)}), bf16[2,768,3072]{2,1,0:T(8,128)(2,1)}) %all-gather.12.cloned.1.call-update) | async-done | bytes 9437200 | tf_op jit(solution)/shard_map/all_gather | solution.py:269
  260.0 3.1 fusion.11
  263.2 78.3 %all-gather.14.cloned.1.call-done = bf16[2,3072,768]{2,1,0:T(8,128)(2,1)} async-done(((bf16[2,192,768]{2,1,0:T(8,128)(2,1)}), bf16[2,3072,768]{2,1,0:T(8,128)(2,1)}) %all-gather.14.cloned.1.call-update) | async-done | bytes 9437200 | tf_op jit(solution)/shard_map/all_gather | solution.py:270
  341.5 3.8 fusion.473
  347.6 3.8 add_convert_fusion.3
  378.7 3.5 fusion.10
  382.3 4.0 fusion.483
  388.7 4.1 add_convert_fusion.2
  420.8 3.3 fusion.3
  424.2 4.5 fusion.468
  434.1 4.6 add_convert_fusion.1
  467.0 3.3 fusion.2
  470.3 4.9 fusion.478
  480.5 5.3 add_convert_fusion
  497.1 2.9 convolution_bitcast_fusion.6
  580.3 2.8 convolution_bitcast_fusion.2
  590.5 4.2 pad_maximum_fusion.3
  597.7 2.5 fusion.433
  602.6 2.9 convolution_add_fusion.2
  605.5 10.6 pad_maximum_fusion.2
  624.7 7.0 pad_maximum_fusion.1
  670.3 6.3 add.638
  682.0 2.5 bitcast_dynamic-update-slice_fusion.1
  692.6 10.2 add.639
  702.8 9.7 pad_maximum_fusion
  717.1 38.9 %all-reduce.1 = bf16[1536]{0:T(1024)(128)(2,1)S(1)} all-reduce(f32[1536]{0:T(1024)S(1)} %pad_maximum_fusion.10), channel_id=8, replica_groups=mesh['dp'=2,'fsdp'=16] {'dp','fsdp'}, use_global_device_ids=true, to_apply=%region_106.107.clone | all-reduce | flops 1536 | bytes 9216
  756.3 3.8 all-reduce
  774.8 2.4 fusion.123
  777.2 2.4 fusion.102
  779.6 2.4 fusion.79
  782.0 2.4 fusion.76
  785.2 3.1 all-gather.2
  789.9 3.1 all-gather.1
  793.7 121.4 %reduce-scatter.13.cloned.1.call-done = f32[2,48,768]{2,1,0:T(8,128)} async-done(((f32[2,1536,768]{2,1,0:T(8,128)}), f32[2,48,768]{2,1,0:T(8,128)}) %reduce-scatter.13.cloned.1.call-update) | async-done | bytes 294928 | tf_op jit(solution)/shard_map/reduce_scatter | solution.py:354
  916.1 4.7 all_gather.57
  921.7 204.7 %reduce-scatter.17.cloned.1.call-done = f32[192,768]{1,0:T(8,128)} async-done(((f32[6144,768]{1,0:T(8,128)}), f32[192,768]{1,0:T(8,128)}) %reduce-scatter.17.cloned.1.call-update) | async-done | bytes 589840 | tf_op jit(solution)/shard_map/reduce_scatter | solution.py:356
  1127.5 7.6 all_gather.59
  1135.2 202.1 %reduce-scatter.15.cloned.1.call-done = f32[48,3072]{1,0:T(8,128)} async-done(((f32[1536,3072]{1,0:T(8,128)}), f32[48,3072]{1,0:T(8,128)}) %reduce-scatter.15.cloned.1.call-update) | async-done | bytes 589840 | tf_op jit(solution)/shard_map/reduce_scatter | solution.py:355
  1338.4 7.8 all_gather.58
  1348.7 258.1 %reduce-scatter.11.cloned.1.call-done = f32[6,48,768]{2,1,0:T(8,128)} async-done(((f32[6,1536,768]{2,1,0:T(8,128)}), f32[6,48,768]{2,1,0:T(8,128)}) %reduce-scatter.11.cloned.1.call-update) | async-done | bytes 884752 | tf_op jit(solution)/shard_map/reduce_scatter | solution.py:353
  1608.0 11.9 all_gather.56
  (1040 shorter events, 316.4 us)
Async XLA Ops:
  7.2 116.9 %all-gather.8.cloned.1.call-start = ((), (), s32[]{:S(2)}) async-start(), calls=%async_computation.6 | async-start | bytes 15040512 | tf_op jit(solution)/shard_map/all_gather | solution.py:267
  7.9 170.4 %all-gather.10.cloned.1.call-start = ((), (), s32[]{:S(2)}) async-start(), calls=%async_computation.7 | async-start | bytes 5013504 | tf_op jit(solution)/shard_map/all_gather | solution.py:268
  8.7 251.3 %all-gather.12.cloned.1.call-start = ((), (), s32[]{:S(2)}) async-start(), calls=%async_computation.8 | async-start | bytes 10027008 | tf_op jit(solution)/shard_map/all_gather | solution.py:269
  9.4 114.7 %copy-start.29 = (bf16[1,20,768]{2,1,0:T(8,128)(2,1)S(1)}, bf16[1,20,768]{2,1,0:T(8,128)(2,1)}, u32[]{:S(2)}) copy-start(bf16[1,20,768]{2,1,0:T(8,128)(2,1)} %param.20) | copy-start | bytes 92164
  9.4 332.1 %all-gather.14.cloned.1.call-start = ((), (), s32[]{:S(2)}) async-start(), calls=%async_computation.9 | async-start | bytes 10027008 | tf_op jit(solution)/shard_map/all_gather | solution.py:270
  10.0 774.4 %reduce-scatter.21.cloned.1.call-start = ((), (), s32[]{:S(2)}) async-start(), calls=%async_computation.15 | async-start | bytes 811008
  76.4 49.3 %copy-start.51 = (bf16[1,48,768]{2,1,0:T(8,128)(2,1)S(1)}, bf16[1,48,768]{2,1,0:T(8,128)(2,1)}, u32[]{:S(2)}) copy-start(bf16[1,48,768]{2,1,0:T(8,128)(2,1)} %param.19) | copy-start | bytes 221188
  92.3 284.4 %copy-start.133 = (f32[768]{0:T(1024)}, f32[768]{0:T(1024)S(1)}, u32[]{:S(2)}) copy-start(f32[768]{0:T(1024)S(1)} %get-tuple-element.77) | copy-start | bytes 9220
  92.3 296.1 %copy-start.137 = (f32[768]{0:T(1024)}, f32[768]{0:T(1024)S(1)}, u32[]{:S(2)}) copy-start(f32[768]{0:T(1024)S(1)} %get-tuple-element.75) | copy-start | bytes 9220
  92.3 302.7 %copy-start.99 = (f32[768]{0:T(1024)}, f32[768]{0:T(1024)S(1)}, u32[]{:S(2)}) copy-start(f32[768]{0:T(1024)S(1)} %get-tuple-element.76) | copy-start | bytes 9220
  105.2 277.0 %copy-start.135 = (f32[768]{0:T(1024)}, f32[768]{0:T(1024)S(1)}, u32[]{:S(2)}) copy-start(f32[768]{0:T(1024)S(1)} %get-tuple-element.79) | copy-start | bytes 9220
  105.2 281.6 %copy-start.147 = (f32[768]{0:T(1024)}, f32[768]{0:T(1024)S(1)}, u32[]{:S(2)}) copy-start(f32[768]{0:T(1024)S(1)} %get-tuple-element.78) | copy-start | bytes 9220
  127.6 58.7 %copy-start.85 = (bf16[48,12,64]{2,1,0:T(8,128)(2,1)}, bf16[48,12,64]{2,1,0:T(8,128)(2,1)S(1)}, u32[]{:S(2)}) copy-start(bf16[48,12,64]{2,1,0:T(8,128)(2,1)S(1)} %reshape.2833) | copy-start | bytes 221188
  129.5 50.8 %copy-start.83 = (bf16[48,12,64]{2,1,0:T(8,128)(2,1)}, bf16[48,12,64]{2,1,0:T(8,128)(2,1)S(1)}, u32[]{:S(2)}) copy-start(bf16[48,12,64]{2,1,0:T(8,128)(2,1)S(1)} %reshape.2835) | copy-start | bytes 221188
  131.8 128.2 %copy-start.113 = (bf16[20,768]{1,0:T(8,128)(2,1)}, bf16[20,768]{1,0:T(8,128)(2,1)S(1)}, u32[]{:S(2)}) copy-start(bf16[20,768]{1,0:T(8,128)(2,1)S(1)} %convert_element_type.1035) | copy-start | bytes 92164
  180.0 83.1 %copy-start.170 = (f32[20]{0:T(128)}, f32[20]{0:T(128)S(1)}, u32[]{:S(2)}) copy-start(f32[20]{0:T(128)S(1)} %broadcast_multiply_fusion.8) | copy-start | bytes 244
  180.2 82.9 %copy-start.260 = (f32[20]{0:T(128)}, f32[20]{0:T(128)S(1)}, u32[]{:S(2)}) copy-start(f32[20]{0:T(128)S(1)} %multiply_reduce_fusion.43) | copy-start | bytes 244
  180.2 82.9 %copy-start.205 = (f32[20]{0:T(128)}, f32[20]{0:T(128)S(1)}, u32[]{:S(2)}) copy-start(f32[20]{0:T(128)S(1)} %fusion.399) | copy-start | bytes 244
  186.7 73.3 %copy-start.115 = (bf16[20,768]{1,0:T(8,128)(2,1)}, bf16[20,768]{1,0:T(8,128)(2,1)S(1)}, u32[]{:S(2)}) copy-start(bf16[20,768]{1,0:T(8,128)(2,1)S(1)} %convert_element_type.1046) | copy-start | bytes 92164
  188.4 165.2 %copy-start.25 = (f32[1,20,768]{2,1,0:T(8,128)}, f32[1,20,768]{2,1,0:T(8,128)S(1)}, u32[]{:S(2)}) copy-start(f32[1,20,768]{2,1,0:T(8,128)S(1)} %get-tuple-element.194) | copy-start | bytes 184324
  188.4 165.1 %copy-start.174 = (f32[20]{0:T(128)}, f32[20]{0:T(128)S(1)}, u32[]{:S(2)}) copy-start(f32[20]{0:T(128)S(1)} %broadcast_multiply_fusion.7) | copy-start | bytes 244
  188.6 165.0 %copy-start.213 = (f32[20]{0:T(128)}, f32[20]{0:T(128)S(1)}, u32[]{:S(2)}) copy-start(f32[20]{0:T(128)S(1)} %fusion.400) | copy-start | bytes 244
  263.1 84.4 %copy-start.27 = (f32[20,3072]{1,0:T(8,128)}, f32[20,3072]{1,0:T(8,128)S(1)}, u32[]{:S(2)}) copy-start(f32[20,3072]{1,0:T(8,128)S(1)} %fusion.11) | copy-start | bytes 737284
  263.1 82.6 %copy-start.112 = (bf16[1,20,768]{2,1,0:T(8,128)(2,1)S(1)}, bf16[1,20,768]{2,1,0:T(8,128)(2,1)}, u32[]{:S(2)}) copy-start(bf16[1,20,768]{2,1,0:T(8,128)(2,1)} %param.28) | copy-start | bytes 92164
  441.2 55.8 %copy-start.249 = (f32[48]{0:T(128)}, f32[48]{0:T(128)S(1)}, u32[]{:S(2)}) copy-start(f32[48]{0:T(128)S(1)} %negate_multiply_fusion.14) | copy-start | bytes 580
  497.1 23.8 %copy-start.169 = (f32[768]{0:T(1024)S(1)}, f32[768]{0:T(1024)}, u32[]{:S(2)}) copy-start(f32[768]{0:T(1024)} %get-tuple-element.105) | copy-start | bytes 9220
  497.1 24.4 %copy-start.168 = (f32[768]{0:T(1024)S(1)}, f32[768]{0:T(1024)}, u32[]{:S(2)}) copy-start(f32[768]{0:T(1024)} %get-tuple-element.121) | copy-start | bytes 9220
  501.9 30.0 %copy-start.15 = (f32[1,28,768]{2,1,0:T(8,128)S(1)}, f32[1,28,768]{2,1,0:T(8,128)}, u32[]{:S(2)}) copy-start(f32[1,28,768]{2,1,0:T(8,128)} %copy-done.14) | copy-start | bytes 258052
  525.6 29.1 %copy-start.94 = (bf16[28,768]{1,0:T(8,128)(2,1)}, bf16[28,768]{1,0:T(8,128)(2,1)S(1)}, u32[]{:S(2)}) copy-start(bf16[28,768]{1,0:T(8,128)(2,1)S(1)} %convert_element_type.1199) | copy-start | bytes 129028
  528.4 26.3 %copy-start.210 = (f32[48]{0:T(128)S(1)}, f32[48]{0:T(128)}, u32[]{:S(2)}) copy-start(f32[48]{0:T(128)} %copy-done.209) | copy-start | bytes 580
  528.4 26.3 %copy-start.229 = (f32[48]{0:T(128)S(1)}, f32[48]{0:T(128)}, u32[]{:S(2)}) copy-start(f32[48]{0:T(128)} %copy-done.228) | copy-start | bytes 580
  530.2 27.1 %copy-start.263 = (f32[48]{0:T(128)S(1)}, f32[48]{0:T(128)}, u32[]{:S(2)}) copy-start(f32[48]{0:T(128)} %copy-done.262) | copy-start | bytes 580
  532.0 26.9 %copy-start.165 = (f32[768]{0:T(1024)S(1)}, f32[768]{0:T(1024)}, u32[]{:S(2)}) copy-start(f32[768]{0:T(1024)} %get-tuple-element.95) | copy-start | bytes 9220
  532.0 28.7 %copy-start.255 = (f32[768]{0:T(1024)S(1)}, f32[768]{0:T(1024)}, u32[]{:S(2)}) copy-start(f32[768]{0:T(1024)} %get-tuple-element.104) | copy-start | bytes 9220
  552.9 21.6 %copy-start.212 = (f32[56]{0:T(128)S(1)}, f32[56]{0:T(128)}, u32[]{:S(2)}) copy-start(f32[56]{0:T(128)} %copy-done.211) | copy-start | bytes 676
  554.7 23.3 %copy-start.179 = (f32[1,768]{1,0:T(1,128)S(1)}, f32[1,768]{1,0:T(1,128)}, u32[]{:S(2)}) copy-start(f32[1,768]{1,0:T(1,128)} %stack.360) | copy-start | bytes 9220
  556.7 21.3 %copy-start.180 = (f32[1,768]{1,0:T(1,128)S(1)}, f32[1,768]{1,0:T(1,128)}, u32[]{:S(2)}) copy-start(f32[1,768]{1,0:T(1,128)} %stack.359) | copy-start | bytes 9220
  556.7 21.3 %copy-start.183 = (f32[1,768]{1,0:T(1,128)S(1)}, f32[1,768]{1,0:T(1,128)}, u32[]{:S(2)}) copy-start(f32[1,768]{1,0:T(1,128)} %stack.358) | copy-start | bytes 9220
  556.7 21.3 %copy-start.185 = (f32[1,768]{1,0:T(1,128)S(1)}, f32[1,768]{1,0:T(1,128)}, u32[]{:S(2)}) copy-start(f32[1,768]{1,0:T(1,128)} %stack.364) | copy-start | bytes 9220
  556.7 21.3 %copy-start.186 = (f32[1,768]{1,0:T(1,128)S(1)}, f32[1,768]{1,0:T(1,128)}, u32[]{:S(2)}) copy-start(f32[1,768]{1,0:T(1,128)} %stack.363) | copy-start | bytes 9220
  556.7 21.4 %copy-start.189 = (f32[1,768]{1,0:T(1,128)S(1)}, f32[1,768]{1,0:T(1,128)}, u32[]{:S(2)}) copy-start(f32[1,768]{1,0:T(1,128)} %stack.352) | copy-start | bytes 9220
  556.7 21.4 %copy-start.190 = (f32[1,768]{1,0:T(1,128)S(1)}, f32[1,768]{1,0:T(1,128)}, u32[]{:S(2)}) copy-start(f32[1,768]{1,0:T(1,128)} %stack.351) | copy-start | bytes 9220
  558.2 26.9 %copy-start.16 = (f32[1,48,768]{2,1,0:T(8,128)}, f32[1,48,768]{2,1,0:T(8,128)S(1)}, u32[]{:S(2)}) copy-start(f32[1,48,768]{2,1,0:T(8,128)S(1)} %get-tuple-element.138) | copy-start | bytes 442372
  579.4 209.6 %reduce-scatter.19.cloned.1.call-start = ((), (), s32[]{:S(2)}) async-start(), calls=%async_computation.14 | async-start | bytes 811008
  584.3 330.8 %reduce-scatter.13.cloned.1.call-start = ((), (), s32[]{:S(2)}) async-start(), calls=%async_computation.11 | async-start | bytes 9732096 | tf_op jit(solution)/shard_map/reduce_scatter | solution.py:354
  594.9 531.6 %reduce-scatter.17.cloned.1.call-start = ((), (), s32[]{:S(2)}) async-start(), calls=%async_computation.13 | async-start | bytes 19464192 | tf_op jit(solution)/shard_map/reduce_scatter | solution.py:356
  616.2 721.1 %reduce-scatter.15.cloned.1.call-start = ((), (), s32[]{:S(2)}) async-start(), calls=%async_computation.12 | async-start | bytes 19464192 | tf_op jit(solution)/shard_map/reduce_scatter | solution.py:355
  631.8 975.0 %reduce-scatter.11.cloned.1.call-start = ((), (), s32[]{:S(2)}) async-start(), calls=%async_computation.10 | async-start | bytes 29196288 | tf_op jit(solution)/shard_map/reduce_scatter | solution.py:353
  (245 other events, 1845.2 us)
Sparse Core Ops, SparseCore 0:
  10.3 113.7 all-gather.7
  126.3 51.9 all-gather.9
  180.6 79.3 all-gather.11
  262.1 79.3 all-gather.13
  579.5 93.5 reduce-scatter.20
  678.6 95.3 reduce-scatter.18
  779.9 135.1 reduce-scatter.12
  921.5 204.8 reduce-scatter.16
  1132.8 204.4 reduce-scatter.14
  1343.6 263.1 reduce-scatter.10
where the time goes:
time: 1650 us; the launch traced here: 1630 us
  waiting for transfers between devices  1000 us (61%)
  matrix products  268 us (16%)
  blocking collectives  143 us (9%)
  local copies, waits for them, and re-layouts  96.1 us (6%)
  other arithmetic  93.7 us (6%)
  between operations  22.9 us (1%)
    reduce_scatter x1, waiting for transfers between devices, per_device(): lax.psum_scatter(packed[0], ('dp', 'fsdp'), scatter_dimension=1, tiled=True)  258 us
    reduce_scatter x1, waiting for transfers between devices, per_device(): lax.psum_scatter(packed[3], ('dp', 'fsdp'), scatter_dimension=0, tiled=True)  205 us
    reduce_scatter x1, waiting for transfers between devices, per_device(): lax.psum_scatter(packed[2], ('dp', 'fsdp'), scatter_dimension=0, tiled=True)  202 us
    reduce_scatter x1, waiting for transfers between devices, per_device(): lax.psum_scatter(packed[1], ('dp', 'fsdp'), scatter_dimension=1, tiled=True)  121 us
    dot_general x40, matrix products, project_back(): jnp.einsum('ple,de->pld', grads, matrix, preferred_element_type=jnp.float32)  85.9 us
    dot_general x40, matrix products, project(): jnp.einsum('pld,de->ple', rows, matrix, preferred_element_type=jnp.float32)  82.7 us
    all_gather x1, waiting for transfers between devices, per_device(): lax.all_gather(ffn_down, 'fsdp', axis=1, tiled=True)  78.3 us
    all_gather x1, waiting for transfers between devices, per_device(): lax.all_gather(ffn_up, 'fsdp', axis=1, tiled=True)  71.4 us
  transfers between devices with their start and end apart: 10, of which 8 were waited for; matrix products, arithmetic and copies ran while one was open for 13% of the time, Pallas kernels for 0%

commit v1 on v0

--- a/solution.py
+++ b/solution.py
@@ -301,15 +301,7 @@
         layouts.append(
             (stream_rows, stream_keys, stream_masks, (cot_text, cot_visual), outputs, saved_list)
         )
-    back_weights = (
-        lax.all_gather(attn_in, "fsdp", axis=2, tiled=True),
-        lax.all_gather(attn_out, "fsdp", axis=2, tiled=True),
-        lax.all_gather(ffn_up, "fsdp", axis=1, tiled=True),
-        lax.all_gather(ffn_down, "fsdp", axis=1, tiled=True),
-        lax.all_gather(norm_gain, "fsdp", axis=2, tiled=True),
-        lax.all_gather(norm_bias, "fsdp", axis=2, tiled=True),
-        lax.all_gather(gate_vector, "fsdp", axis=1, tiled=True),
-    )
+    back_weights = gathered
     input_grads = [[None, None], [None, None]]
     stream_grads = []
     for stream in (0, 1):
@@ -349,37 +341,16 @@
             for index in range(7)
         )
     )
-    shares = (
-        lax.psum_scatter(packed[0], ("dp", "fsdp"), scatter_dimension=1, tiled=True),
-        lax.psum_scatter(packed[1], ("dp", "fsdp"), scatter_dimension=1, tiled=True),
-        lax.psum_scatter(packed[2], ("dp", "fsdp"), scatter_dimension=0, tiled=True),
-        lax.psum_scatter(packed[3], ("dp", "fsdp"), scatter_dimension=0, tiled=True),
-        lax.psum_scatter(packed[4], ("dp", "fsdp"), scatter_dimension=1, tiled=True),
-        lax.psum_scatter(packed[5], ("dp", "fsdp"), scatter_dimension=1, tiled=True),
-        lax.psum_scatter(packed[6], ("dp", "fsdp"), scatter_dimension=0, tiled=True),
-    )
-    joined = (
-        lax.all_gather(shares[0].astype(jnp.bfloat16), "dp", axis=1, tiled=True).astype(
-            jnp.float32
-        ),
-        lax.all_gather(shares[1].astype(jnp.bfloat16), "dp", axis=1, tiled=True).astype(
-            jnp.float32
-        ),
-        lax.all_gather(shares[2].astype(jnp.bfloat16), "dp", axis=0, tiled=True).astype(
-            jnp.float32
-        ),
-        lax.all_gather(shares[3].astype(jnp.bfloat16), "dp", axis=0, tiled=True).astype(
-            jnp.float32
-        ),
-        lax.all_gather(shares[4].astype(jnp.bfloat16), "dp", axis=1, tiled=True).astype(
-            jnp.float32
-        ),
-        lax.all_gather(shares[5].astype(jnp.bfloat16), "dp", axis=1, tiled=True).astype(
-            jnp.float32
-        ),
-        lax.all_gather(shares[6].astype(jnp.bfloat16), "dp", axis=0, tiled=True).astype(
-            jnp.float32
-        ),
+    axes = ("dp", "fsdp")
+    shares = tuple(
+        lax.psum_scatter(
+            packed[index].astype(jnp.bfloat16), axes, scatter_dimension=row_dims[index], tiled=True
+        )
+        for index in range(7)
+    )
+    joined = tuple(
+        lax.all_gather(shares[index], "dp", axis=row_dims[index], tiled=True).astype(jnp.float32)
+        for index in range(7)
     )
     finals = tuple(
         (jnp.stack(jnp.split(joined[index], 2, axis=row_dims[index])) for index in range(7))

time: 1650 us -> 1370 us (0.83)
  waiting for transfers between devices: 1000 us -> 741 us
    reduce_scatter x4, waiting for transfers between devices: 786 us -> 523 us  [per_device(): lax.psum_scatter(packed[index].astype(jnp.bfloat16), axes, scatter_dimens...]
    another operation x6 -> x16, other arithmetic: 1.72 us -> 22.7 us
    add x10 -> x0, other arithmetic: 18.5 us -> none  [per_device(): summed = tuple((left + right for left, right in zip(summed, grads_here)))]
  transfers between devices with their start and end apart: 10 -> 10, of which waited for: 8 -> 8; matrix products, arithmetic and copies ran while one was open for 13% -> 15% of each run, Pallas kernels for 0% -> 0%
where the time goes in v1:
time: 1370 us; the launch traced here: 1350 us
  waiting for transfers between devices  741 us (54%)
  matrix products  258 us (19%)
  blocking collectives  141 us (10%)
  local copies, waits for them, and re-layouts  98.9 us (7%)
  other arithmetic  92.2 us (7%)
  between operations  22.6 us (2%)
    reduce_scatter x4, waiting for transfers between devices, per_device(): lax.psum_scatter(packed[index].astype(jnp.bfloat16), axes, scatter_dimens...  523 us
    dot_general x40, matrix products, project_back(): jnp.einsum('ple,de->pld', grads, matrix, preferred_element_type=jnp.float32)  86.2 us
    dot_general x40, matrix products, project(): jnp.einsum('pld,de->ple', rows, matrix, preferred_element_type=jnp.float32)  82.6 us
    all_gather x1, waiting for transfers between devices, per_device(): lax.all_gather(ffn_down, 'fsdp', axis=1, tiled=True)  78.3 us
    all_gather x1, waiting for transfers between devices, per_device(): lax.all_gather(ffn_up, 'fsdp', axis=1, tiled=True)  71.4 us
    dot_general x40, matrix products, weight_grad(): jnp.einsum('pld,ple->de', rows, grads, preferred_element_type=jnp.float32)  52 us
    all_gather x1, waiting for transfers between devices, per_device(): lax.all_gather(attn_out, 'fsdp', axis=2, tiled=True)  46.7 us
    unnamed x2, blocking collectives  43 us
  transfers between devices with their start and end apart: 10, of which 8 were waited for; matrix products, arithmetic and copies ran while one was open for 15% of the time, Pallas kernels for 0%

profile of v1, /device:TPU:31, one launch (start us, length us, event | category | flops | bytes accessed | tf_op | source)
XLA Modules:
  0.0 1354.8 jit_solution(2017214899747914413)
XLA Ops:
  12.6 17.3 %all-gather = bf16[16,48,2]{1,2,0:T(2,128)(2,1)S(1)} all-gather(bf16[1,48,2]{1,2,0:T(2,128)(2,1)} %bitcast.1037), channel_id=1, replica_groups=mesh['dp'=2,'fsdp'=16] {'fsdp'}, dimensions={0}, use_global_device_ids=true | all-gather | bytes 3264 | tf_op jit(solution)/shard_map/all_gather | solution.py:273
  33.0 22.3 %all_gather.45 = bf16[2,3,768]{1,0,2:T(2,128)(2,1)S(1)} all-gather(bf16[2,3,48]{1,0,2:T(2,128)(2,1)S(1)} %copy.440), channel_id=1, replica_groups=mesh['dp'=2,'fsdp'=16] {'fsdp'}, dimensions={2}, use_global_device_ids=true | all-gather | bytes 9792 | tf_op jit(solution)/shard_map/all_gather | solution.py:272
  55.3 21.9 %all_gather.44 = bf16[2,3,768]{1,0,2:T(2,128)(2,1)S(1)} all-gather(bf16[2,3,48]{1,0,2:T(2,128)(2,1)S(1)} %copy.439), channel_id=1, replica_groups=mesh['dp'=2,'fsdp'=16] {'fsdp'}, dimensions={2}, use_global_device_ids=true | all-gather | bytes 9792 | tf_op jit(solution)/shard_map/all_gather | solution.py:271
  79.9 12.5 slice_reduce_fusion.1
  92.4 13.0 slice_reduce_fusion
  105.4 19.2 %all-gather.8.cloned.1.call-done = bf16[2,6,768,768]{3,2,1,0:T(8,128)(2,1)} async-done(((bf16[2,6,48,768]{3,2,1,0:T(8,128)(2,1)}), bf16[2,6,768,768]{3,2,1,0:T(8,128)(2,1)}) %all-gather.8.cloned.1.call-update) | async-done | bytes 14155792 | tf_op jit(solution)/shard_map/all_gather | solution.py:267
  131.9 46.7 %all-gather.10.cloned.1.call-done = bf16[2,2,768,768]{3,2,1,0:T(8,128)(2,1)} async-done(((bf16[2,2,48,768]{3,2,1,0:T(8,128)(2,1)}), bf16[2,2,768,768]{3,2,1,0:T(8,128)(2,1)}) %all-gather.10.cloned.1.call-update) | async-done | bytes 4718608 | tf_op jit(solution)/shard_map/all_gather | solution.py:268
  188.9 71.4 %all-gather.12.cloned.1.call-done = bf16[2,768,3072]{2,1,0:T(8,128)(2,1)} async-done(((bf16[2,48,3072]{2,1,0:T(8,128)(2,1)}), bf16[2,768,3072]{2,1,0:T(8,128)(2,1)}) %all-gather.12.cloned.1.call-update) | async-done | bytes 9437200 | tf_op jit(solution)/shard_map/all_gather | solution.py:269
  260.3 3.1 fusion.13
  263.4 78.3 %all-gather.14.cloned.1.call-done = bf16[2,3072,768]{2,1,0:T(8,128)(2,1)} async-done(((bf16[2,192,768]{2,1,0:T(8,128)(2,1)}), bf16[2,3072,768]{2,1,0:T(8,128)(2,1)}) %all-gather.14.cloned.1.call-update) | async-done | bytes 9437200 | tf_op jit(solution)/shard_map/all_gather | solution.py:270
  341.8 3.8 fusion.479
  348.6 3.8 add_convert_fusion.9
  378.5 3.5 fusion.12
  382.1 4.0 fusion.489
  389.1 4.1 add_convert_fusion.8
  420.7 3.3 fusion.5
  424.1 4.5 fusion.474
  434.0 4.6 add_convert_fusion.7
  466.0 3.3 fusion.4
  469.4 4.9 fusion.484
  479.5 5.3 add_convert_fusion.6
  582.2 2.8 convolution_bitcast_fusion.2
  593.6 2.5 pad_maximum_fusion.3
  599.0 2.5 fusion.439
  603.9 3.1 add_convert_fusion.3
  606.9 15.5 %pad_maximum_fusion.2 = bf16[6144,768]{1,0:T(8,128)(2,1)} fusion(bf16[3072,768]{1,0:T(8,128)(2,1)S(1)} %add_convert_fusion.2, bf16[3072,768]{1,0:T(8,128)(2,1)S(1)} %add_convert_fusion.3), kind=kLoop, calls=%fused_computation.4 | loop fusion | flops 18874368 | bytes 18874368 | tf_op jit(solution)/shard_map/concatenate | solution.py:340
  648.3 4.4 pad_maximum_fusion.1
  666.9 2.6 bitcast_dynamic-update-slice_fusion.7
  675.7 2.6 bitcast_dynamic-update-slice_fusion.19
  681.7 9.9 add_convert_fusion.1
  691.6 6.2 add_convert_fusion
  697.9 10.1 pad_maximum_fusion
  712.5 38.8 %all-reduce.1 = bf16[1536]{0:T(1024)(128)(2,1)S(1)} all-reduce(bf16[1536]{0:T(1024)(128)(2,1)S(1)} %pad_maximum_fusion.12), channel_id=8, replica_groups=mesh['dp'=2,'fsdp'=16] {'dp','fsdp'}, use_global_device_ids=true, to_apply=%region_106.107.clone | all-reduce | flops 1536 | bytes 6144
  751.6 4.2 all-reduce
  770.5 2.4 fusion.125
  772.9 2.4 fusion.104
  775.3 2.4 fusion.81
  777.7 2.4 fusion.78
  780.9 3.1 all-gather.2
  785.6 3.1 all-gather.1
  789.4 96.2 %reduce-scatter.13.cloned.1.call-done = bf16[2,48,768]{2,1,0:T(8,128)(2,1)} async-done(((bf16[2,1536,768]{2,1,0:T(8,128)(2,1)}), bf16[2,48,768]{2,1,0:T(8,128)(2,1)}) %reduce-scatter.13.cloned.1.call-update) | async-done | bytes 147472 | tf_op jit(solution)/shard_map/reduce_scatter | solution.py:346
  885.5 4.9 all_gather.50
  891.3 135.6 %reduce-scatter.17.cloned.1.call-done = bf16[192,768]{1,0:T(8,128)(2,1)} async-done(((bf16[6144,768]{1,0:T(8,128)(2,1)}), bf16[192,768]{1,0:T(8,128)(2,1)}) %reduce-scatter.17.cloned.1.call-update) | async-done | bytes 294928 | tf_op jit(solution)/shard_map/reduce_scatter | solution.py:346
  1027.0 7.7 all_gather.52
  1034.7 133.6 %reduce-scatter.15.cloned.1.call-done = bf16[48,3072]{1,0:T(8,128)(2,1)} async-done(((bf16[1536,3072]{1,0:T(8,128)(2,1)}), bf16[48,3072]{1,0:T(8,128)(2,1)}) %reduce-scatter.15.cloned.1.call-update) | async-done | bytes 294928 | tf_op jit(solution)/shard_map/reduce_scatter | solution.py:346
  1168.4 7.7 all_gather.51
  1178.5 157.5 %reduce-scatter.11.cloned.1.call-done = bf16[6,48,768]{2,1,0:T(8,128)(2,1)} async-done(((bf16[6,1536,768]{2,1,0:T(8,128)(2,1)}), bf16[6,48,768]{2,1,0:T(8,128)(2,1)}) %reduce-scatter.11.cloned.1.call-update) | async-done | bytes 442384 | tf_op jit(solution)/shard_map/reduce_scatter | solution.py:346
  1336.0 10.2 all_gather.49
  (986 shorter events, 307.1 us)
Async XLA Ops:
  7.2 117.4 %all-gather.8.cloned.1.call-start = ((), (), s32[]{:S(2)}) async-start(), calls=%async_computation.6 | async-start | bytes 15040512 | tf_op jit(solution)/shard_map/all_gather | solution.py:267
  7.9 170.7 %all-gather.10.cloned.1.call-start = ((), (), s32[]{:S(2)}) async-start(), calls=%async_computation.7 | async-start | bytes 5013504 | tf_op jit(solution)/shard_map/all_gather | solution.py:268
  8.7 251.6 %all-gather.12.cloned.1.call-start = ((), (), s32[]{:S(2)}) async-start(), calls=%async_computation.8 | async-start | bytes 10027008 | tf_op jit(solution)/shard_map/all_gather | solution.py:269
  9.4 115.2 %copy-start.22 = (bf16[1,20,768]{2,1,0:T(8,128)(2,1)S(1)}, bf16[1,20,768]{2,1,0:T(8,128)(2,1)}, u32[]{:S(2)}) copy-start(bf16[1,20,768]{2,1,0:T(8,128)(2,1)} %param.20) | copy-start | bytes 92164
  9.4 332.4 %all-gather.14.cloned.1.call-start = ((), (), s32[]{:S(2)}) async-start(), calls=%async_computation.9 | async-start | bytes 10027008 | tf_op jit(solution)/shard_map/all_gather | solution.py:270
  10.0 770.1 %reduce-scatter.21.cloned.1.call-start = ((), (), s32[]{:S(2)}) async-start(), calls=%async_computation.15 | async-start | bytes 405504
  31.4 401.7 %copy-start.132 = (f32[768]{0:T(1024)}, f32[768]{0:T(1024)S(1)}, u32[]{:S(2)}) copy-start(f32[768]{0:T(1024)S(1)} %convert.50) | copy-start | bytes 9220
  77.2 49.1 %copy-start.44 = (bf16[1,48,768]{2,1,0:T(8,128)(2,1)S(1)}, bf16[1,48,768]{2,1,0:T(8,128)(2,1)}, u32[]{:S(2)}) copy-start(bf16[1,48,768]{2,1,0:T(8,128)(2,1)} %param.19) | copy-start | bytes 221188
  78.2 288.5 %copy-start.155 = (pred[56]{0:T(512)(128)(4,1)}, pred[56]{0:T(512)(128)(4,1)S(1)}, u32[]{:S(2)}) copy-start(pred[56]{0:T(512)(128)(4,1)S(1)} %iota_compare_fusion) | copy-start | bytes 172
  92.4 296.4 %copy-start.120 = (f32[768]{0:T(1024)}, f32[768]{0:T(1024)S(1)}, u32[]{:S(2)}) copy-start(f32[768]{0:T(1024)S(1)} %get-tuple-element.75) | copy-start | bytes 9220
  92.4 371.6 %copy-start.118 = (f32[768]{0:T(1024)}, f32[768]{0:T(1024)S(1)}, u32[]{:S(2)}) copy-start(f32[768]{0:T(1024)S(1)} %get-tuple-element.250) | copy-start | bytes 9220
  105.4 281.8 %copy-start.137 = (f32[768]{0:T(1024)}, f32[768]{0:T(1024)S(1)}, u32[]{:S(2)}) copy-start(f32[768]{0:T(1024)S(1)} %get-tuple-element.78) | copy-start | bytes 9220
  105.4 324.4 %copy-start.134 = (f32[768]{0:T(1024)}, f32[768]{0:T(1024)S(1)}, u32[]{:S(2)}) copy-start(f32[768]{0:T(1024)S(1)} %get-tuple-element.249) | copy-start | bytes 9220
  128.1 57.4 %copy-start.76 = (bf16[48,12,64]{2,1,0:T(8,128)(2,1)}, bf16[48,12,64]{2,1,0:T(8,128)(2,1)S(1)}, u32[]{:S(2)}) copy-start(bf16[48,12,64]{2,1,0:T(8,128)(2,1)S(1)} %reshape.2833) | copy-start | bytes 221188
  130.0 50.5 %copy-start.74 = (bf16[48,12,64]{2,1,0:T(8,128)(2,1)}, bf16[48,12,64]{2,1,0:T(8,128)(2,1)S(1)}, u32[]{:S(2)}) copy-start(bf16[48,12,64]{2,1,0:T(8,128)(2,1)S(1)} %reshape.2835) | copy-start | bytes 221188
  130.9 57.7 %copy-start.139 = (f32[12,20]{1,0:T(8,128)}, f32[12,20]{1,0:T(8,128)S(1)}, u32[]{:S(2)}) copy-start(f32[12,20]{1,0:T(8,128)S(1)} %get-tuple-element.187) | copy-start | bytes 2884
  131.5 57.1 %copy-start.141 = (f32[12,20]{1,0:T(8,128)}, f32[12,20]{1,0:T(8,128)S(1)}, u32[]{:S(2)}) copy-start(f32[12,20]{1,0:T(8,128)S(1)} %fusion.204) | copy-start | bytes 2884
  131.9 131.5 %copy-start.101 = (bf16[20,768]{1,0:T(8,128)(2,1)}, bf16[20,768]{1,0:T(8,128)(2,1)S(1)}, u32[]{:S(2)}) copy-start(bf16[20,768]{1,0:T(8,128)(2,1)S(1)} %convert_element_type.1021) | copy-start | bytes 92164
  180.3 80.0 %copy-start.166 = (f32[20]{0:T(128)}, f32[20]{0:T(128)S(1)}, u32[]{:S(2)}) copy-start(f32[20]{0:T(128)S(1)} %broadcast_multiply_fusion.8) | copy-start | bytes 244
  180.5 79.8 %copy-start.183 = (f32[20]{0:T(128)}, f32[20]{0:T(128)S(1)}, u32[]{:S(2)}) copy-start(f32[20]{0:T(128)S(1)} %fusion.405) | copy-start | bytes 244
  180.6 82.8 %copy-start.24 = (bf16[20,768]{1,0:T(8,128)(2,1)}, bf16[20,768]{1,0:T(8,128)(2,1)S(1)}, u32[]{:S(2)}) copy-start(bf16[20,768]{1,0:T(8,128)(2,1)S(1)} %fusion.372) | copy-start | bytes 92164
  186.9 158.7 %copy-start.103 = (bf16[20,768]{1,0:T(8,128)(2,1)}, bf16[20,768]{1,0:T(8,128)(2,1)S(1)}, u32[]{:S(2)}) copy-start(bf16[20,768]{1,0:T(8,128)(2,1)S(1)} %convert_element_type.1032) | copy-start | bytes 92164
  188.6 165.9 %copy-start.18 = (f32[1,20,768]{2,1,0:T(8,128)}, f32[1,20,768]{2,1,0:T(8,128)S(1)}, u32[]{:S(2)}) copy-start(f32[1,20,768]{2,1,0:T(8,128)S(1)} %get-tuple-element.194) | copy-start | bytes 184324
  188.6 165.9 %copy-start.167 = (f32[20]{0:T(128)}, f32[20]{0:T(128)S(1)}, u32[]{:S(2)}) copy-start(f32[20]{0:T(128)S(1)} %broadcast_multiply_fusion.7) | copy-start | bytes 244
  188.8 165.7 %copy-start.190 = (f32[20]{0:T(128)}, f32[20]{0:T(128)S(1)}, u32[]{:S(2)}) copy-start(f32[20]{0:T(128)S(1)} %fusion.406) | copy-start | bytes 244
  263.4 85.2 %copy-start.20 = (f32[20,3072]{1,0:T(8,128)}, f32[20,3072]{1,0:T(8,128)S(1)}, u32[]{:S(2)}) copy-start(f32[20,3072]{1,0:T(8,128)S(1)} %fusion.13) | copy-start | bytes 737284
  263.4 83.3 %copy-start.100 = (bf16[1,20,768]{2,1,0:T(8,128)(2,1)S(1)}, bf16[1,20,768]{2,1,0:T(8,128)(2,1)}, u32[]{:S(2)}) copy-start(bf16[1,20,768]{2,1,0:T(8,128)(2,1)} %param.28) | copy-start | bytes 92164
  354.7 153.3 %copy-start.41 = (f32[1,20,768]{2,1,0:T(8,128)}, f32[1,20,768]{2,1,0:T(8,128)S(1)}, u32[]{:S(2)}) copy-start(f32[1,20,768]{2,1,0:T(8,128)S(1)} %get-tuple-element.146) | copy-start | bytes 184324
  378.3 17.2 %copy-start.26 = (f32[1,28,768]{2,1,0:T(8,128)}, f32[1,28,768]{2,1,0:T(8,128)S(1)}, u32[]{:S(2)}) copy-start(f32[1,28,768]{2,1,0:T(8,128)S(1)} %get-tuple-element.218) | copy-start | bytes 258052
  378.3 17.2 %copy-start.171 = (f32[28]{0:T(128)}, f32[28]{0:T(128)S(1)}, u32[]{:S(2)}) copy-start(f32[28]{0:T(128)S(1)} %broadcast_multiply_fusion.1) | copy-start | bytes 340
  378.5 17.0 %copy-start.192 = (f32[28]{0:T(128)}, f32[28]{0:T(128)S(1)}, u32[]{:S(2)}) copy-start(f32[28]{0:T(128)S(1)} %fusion.412) | copy-start | bytes 340
  420.5 20.4 %copy-start.164 = (f32[48]{0:T(128)}, f32[48]{0:T(128)S(1)}, u32[]{:S(2)}) copy-start(f32[48]{0:T(128)S(1)} %broadcast_multiply_fusion.10) | copy-start | bytes 580
  420.7 20.2 %copy-start.181 = (f32[48]{0:T(128)}, f32[48]{0:T(128)S(1)}, u32[]{:S(2)}) copy-start(f32[48]{0:T(128)S(1)} %fusion.403) | copy-start | bytes 580
  441.1 53.5 %copy-start.11 = (f32[1,48,768]{2,1,0:T(8,128)}, f32[1,48,768]{2,1,0:T(8,128)S(1)}, u32[]{:S(2)}) copy-start(f32[1,48,768]{2,1,0:T(8,128)S(1)} %get-tuple-element.140) | copy-start | bytes 442372
  441.1 53.5 %copy-start.223 = (f32[48]{0:T(128)}, f32[48]{0:T(128)S(1)}, u32[]{:S(2)}) copy-start(f32[48]{0:T(128)S(1)} %negate_multiply_fusion.14) | copy-start | bytes 580
  465.8 21.3 %copy-start.7 = (f32[1,56,768]{2,1,0:T(8,128)}, f32[1,56,768]{2,1,0:T(8,128)S(1)}, u32[]{:S(2)}) copy-start(f32[1,56,768]{2,1,0:T(8,128)S(1)} %get-tuple-element.206) | copy-start | bytes 516100
  465.8 21.3 %copy-start.187 = (f32[56]{0:T(128)}, f32[56]{0:T(128)S(1)}, u32[]{:S(2)}) copy-start(f32[56]{0:T(128)S(1)} %broadcast_multiply_fusion.4) | copy-start | bytes 676
  466.0 21.1 %copy-start.213 = (f32[56]{0:T(128)}, f32[56]{0:T(128)S(1)}, u32[]{:S(2)}) copy-start(f32[56]{0:T(128)S(1)} %fusion.409) | copy-start | bytes 676
  469.4 15.5 %slice-start.9 = ((s8[9437184]{0:T(1024)(128)(4,1)}), s8[4194304]{0:T(1024)(128)(4,1)S(1)}, s32[]{:S(2)}) async-start(s8[9437184]{0:T(1024)(128)(4,1)} %bitcast.1027), calls=%async_computation.25 | async-start | bytes 8388608
  469.4 15.5 %slice-start.10 = ((s8[9437184]{0:T(1024)(128)(4,1)}), s8[4194304]{0:T(1024)(128)(4,1)S(1)}, s32[]{:S(2)}) async-start(s8[9437184]{0:T(1024)(128)(4,1)} %bitcast.1027), calls=%async_computation.26 | async-start | bytes 8388608
  516.0 22.2 %copy-start.10 = (f32[1,28,768]{2,1,0:T(8,128)S(1)}, f32[1,28,768]{2,1,0:T(8,128)}, u32[]{:S(2)}) copy-start(f32[1,28,768]{2,1,0:T(8,128)} %copy-done.9) | copy-start | bytes 258052
  524.9 20.1 %copy-start.86 = (bf16[28,768]{1,0:T(8,128)(2,1)}, bf16[28,768]{1,0:T(8,128)(2,1)S(1)}, u32[]{:S(2)}) copy-start(bf16[28,768]{1,0:T(8,128)(2,1)S(1)} %convert_element_type.1185) | copy-start | bytes 129028
  569.1 16.9 %copy-start.52 = (bf16[56,768]{1,0:T(8,128)(2,1)}, bf16[56,768]{1,0:T(8,128)(2,1)S(1)}, u32[]{:S(2)}) copy-start(bf16[56,768]{1,0:T(8,128)(2,1)S(1)} %convert_element_type.1168) | copy-start | bytes 258052
  580.7 204.1 %reduce-scatter.19.cloned.1.call-start = ((), (), s32[]{:S(2)}) async-start(), calls=%async_computation.14 | async-start | bytes 405504
  586.1 299.5 %reduce-scatter.13.cloned.1.call-start = ((), (), s32[]{:S(2)}) async-start(), calls=%async_computation.11 | async-start | bytes 4866048 | tf_op jit(solution)/shard_map/reduce_scatter | solution.py:346
  596.2 430.8 %reduce-scatter.17.cloned.1.call-start = ((), (), s32[]{:S(2)}) async-start(), calls=%async_computation.13 | async-start | bytes 9732096 | tf_op jit(solution)/shard_map/reduce_scatter | solution.py:346
  622.6 545.8 %reduce-scatter.15.cloned.1.call-start = ((), (), s32[]{:S(2)}) async-start(), calls=%async_computation.12 | async-start | bytes 9732096 | tf_op jit(solution)/shard_map/reduce_scatter | solution.py:346
  652.7 683.3 %reduce-scatter.11.cloned.1.call-start = ((), (), s32[]{:S(2)}) async-start(), calls=%async_computation.10 | async-start | bytes 14598144 | tf_op jit(solution)/shard_map/reduce_scatter | solution.py:346
  (220 other events, 1356.9 us)
Sparse Core Ops, SparseCore 0:
  10.3 114.2 all-gather.7
  126.9 51.6 all-gather.9
  180.9 79.3 all-gather.11
  262.4 79.3 all-gather.13
  580.8 92.8 reduce-scatter.20
  679.1 94.8 reduce-scatter.18
  779.4 106.0 reduce-scatter.12
  891.4 135.4 reduce-scatter.16
  1032.9 135.4 reduce-scatter.14
  1174.2 161.7 reduce-scatter.10

commit v2 on v0

--- a/solution.py
+++ b/solution.py
@@ -4,9 +4,58 @@
 import jax
 import jax.numpy as jnp
 from jax import lax
+from jax.experimental import pallas as pl
+from jax.experimental.pallas import tpu as pltpu
 from jax.sharding import PartitionSpec as P
 
 HEADS = 12
+BF = jnp.bfloat16
+F32 = jnp.float32
+MESH_ID = pl.DeviceIdType.MESH
+NEG = -1000000000.0
+
+
+def dot(a, b):
+    return lax.dot_general(a, b, (((1,), (0,)), ((), ())), preferred_element_type=F32)
+
+
+def dot_rt(a, b):
+    return lax.dot_general(a, b, (((1,), (1,)), ((), ())), preferred_element_type=F32)
+
+
+def dot_lt(a, b):
+    return lax.dot_general(a, b, (((0,), (0,)), ((), ())), preferred_element_type=F32)
+
+
+def loop(count, body):
+    def step(index, carry):
+        body(index)
+        return carry
+
+    lax.fori_loop(0, count, step, 0)
+
+
+def cols(index, size):
+    return pl.ds(pl.multiple_of(index * size, size), size)
+
+
+def erf_of(value):
+    x = jnp.minimum(jnp.maximum(value, -3.832506856900711), 3.832506856900711)
+    y = x * x
+    top = jnp.full_like(y, 0.00022905065861350646)
+    for c in (0.0034082910107109506, 0.050955695062380861, 0.18520832239976145, 1.128379143519084):
+        top = top * y + c
+    low = jnp.full_like(y, -1.1791602954361697e-7)
+    for c in (
+        0.000023547966471313185,
+        0.0010179625278914885,
+        0.014070470171167667,
+        0.11098505178285362,
+        0.49746925110067538,
+        1.0,
+    ):
+        low = low * y + c
+    return x * top / low
 
 
 def project(rows, matrix):
@@ -242,7 +291,7 @@
     )
 
 
-def per_device(
+def plain_path(
     text_a,
     visual_a,
     text_b,
@@ -301,15 +350,7 @@
         layouts.append(
             (stream_rows, stream_keys, stream_masks, (cot_text, cot_visual), outputs, saved_list)
         )
-    back_weights = (
-        lax.all_gather(attn_in, "fsdp", axis=2, tiled=True),
-        lax.all_gather(attn_out, "fsdp", axis=2, tiled=True),
-        lax.all_gather(ffn_up, "fsdp", axis=1, tiled=True),
-        lax.all_gather(ffn_down, "fsdp", axis=1, tiled=True),
-        lax.all_gather(norm_gain, "fsdp", axis=2, tiled=True),
-        lax.all_gather(norm_bias, "fsdp", axis=2, tiled=True),
-        lax.all_gather(gate_vector, "fsdp", axis=1, tiled=True),
-    )
+    back_weights = gathered
     input_grads = [[None, None], [None, None]]
     stream_grads = []
     for stream in (0, 1):
@@ -405,7 +446,964 @@
     )
 
 
+class Geometry:
+    def __init__(self, mesh, shapes):
+        self.dp = mesh.shape["dp"]
+        self.fsdp = mesh.shape["fsdp"]
+        (self.la, self.lva), (self.lb, self.lvb) = (
+            (shapes[0][1], shapes[1][1]),
+            (shapes[2][1], shapes[3][1]),
+        )
+        self.d = shapes[0][2]
+        self.rows = self.d // self.fsdp
+        self.ff = shapes[14][2]
+        self.pages = shapes[0][0]
+        self.t0 = -(-(self.la + self.lb) // 16) * 16
+        self.t1 = -(-(self.lva + self.lvb) // 16) * 16
+        self.t = self.t0 + self.t1
+        self.nz = self.fsdp // 4
+
+    def fits(self):
+        return (
+            self.dp == 2
+            and self.fsdp == 16
+            and self.pages == 1
+            and self.d == 16 * 48
+            and self.ff == 4 * self.d
+            and self.t0 >= self.t1
+            and self.d == 64 * HEADS
+        )
+
+
+def layer_kernel(g, *refs):
+    D, FF, R, T0, T1, T, NZ = g.d, g.ff, g.rows, g.t0, g.t1, g.t, g.nz
+    ZR = D // NZ
+    it = iter(refs)
+    take = lambda n: [next(it) for _ in range(n)]
+    lens = take(4)
+    rows_in = take(4)
+    cots_in = take(4)
+    w_parts = take(4)
+    (vec_in,) = take(1)
+    outs = take(4)
+    grads = take(4)
+    ga, gu, gd, vec_out = take(4)
+    ra, rg, rfa, rfg = take(4)
+    W, VEC, vecs = take(3)
+    S, A, DU, CQ, SQ, DO = take(6)
+    RES, HID, DR, XH, RSTD, GP = take(6)
+    p_refs = take(4)
+    RZ, FB, VG, VR, VZ = take(5)
+    (s_loc, s_vec, r_vec, sz, rz, sy, ry, sx, rx, sc, rc) = take(11)
+    (s_ex, r_ex, s_own, s_st, s_zr, r_zr, s_rd, r_rd, s_vg, r_vg, s_vz, r_vz) = take(12)
+
+    X, H1, OC, OS, H2 = 0, 1, 2, 3, 4
+    DQC, DKC, DVC, DQS, DKS, DVS, DC, DS, DF = range(5, 14)
+    span = (slice(0, T0), slice(T0, T))
+    size = (T0, T1)
+
+    x = lax.axis_index("dp")
+    f = lax.axis_index("fsdp")
+    z, y, c = f // 4, (f // 2) % 2, f % 2
+    me = x * 4 + y * 2 + c
+
+    def device(xx, zz, yy, cc):
+        return (xx, zz * 4 + yy * 2 + cc)
+
+    def role_device(r):
+        return device(r // 4, z, (r // 2) % 2, r % 2)
+
+    def remote(src, dst, send, recv, dev):
+        return pltpu.make_async_remote_copy(
+            src_ref=src, dst_ref=dst, send_sem=send, recv_sem=recv, device_id=dev,
+            device_id_type=MESH_ID,
+        )
+
+    barrier = pltpu.get_barrier_semaphore()
+    for step in range(1, g.fsdp):
+        pl.semaphore_signal(
+            barrier, inc=1, device_id=(x, (f + step) % g.fsdp), device_id_type=MESH_ID
+        )
+    for r in range(4):
+        pl.semaphore_signal(
+            barrier, inc=1, device_id=device(1 - x, z, r // 2, r % 2), device_id_type=MESH_ID
+        )
+    pl.semaphore_wait(barrier, g.fsdp + 3)
+
+    def wref(k, ff, r0, n):
+        down = k // 12
+        unit = k + down * (12 + (4 * R * ff) // D - k)
+        row = R * ff + down * ((4 * R * ff) % D + R * (k - 12) - R * ff) + r0
+        return W.at[:, unit, pl.ds(pl.multiple_of(row, 16), n)]
+
+    def local_part(k):
+        w_in, w_out, w_up, w_dn = w_parts
+        if k in (3, 7):
+            return w_out.at[:, (k - 3) // 4]
+        if k < 8:
+            return w_in.at[:, (0, 1, 2, None, 3, 4, 5)[k]]
+        if k < 12:
+            return w_up.at[:, :, pl.ds(D * (k - 8), D)]
+        return w_dn.at[:, pl.ds(R * (k - 12), R)]
+
+    third = R // 3
+    local = []
+    for k in range(16):
+        cp = pltpu.make_async_copy(local_part(k), wref(k, f, 0, R), s_loc.at[k])
+        cp.start()
+        local.append(cp)
+
+    def vec_copy(step):
+        return remote(
+            vec_in, VEC.at[f], s_vec.at[step - 1], r_vec.at[step - 1],
+            (x, (f + step) % g.fsdp),
+        )
+
+    def vec_wait(step):
+        ref = VEC.at[(f + g.fsdp - step) % g.fsdp]
+        remote(ref, ref, s_vec.at[step - 1], r_vec.at[step - 1], (x, f)).wait_recv()
+
+    for step in range(1, g.fsdp):
+        vec_copy(step).start()
+    own_vec = pltpu.make_async_copy(vec_in, VEC.at[f], s_loc.at[16])
+    own_vec.start()
+
+    def shard(zz, yy):
+        return zz * 4 + yy * 2 + c
+
+    def z_copy(k, d):
+        ref = wref(k, f, third * x, 2 * third)
+        return remote(ref, ref, sz.at[k, d - 1], rz.at[k, d - 1], device(x, (z + d) % NZ, y, c))
+
+    def z_wait(k, d):
+        ref = wref(k, shard((z + NZ - d) % NZ, y), third * x, 2 * third)
+        remote(ref, ref, sz.at[k, d - 1], rz.at[k, d - 1], device(x, (z + d) % NZ, y, c)).wait_recv()
+
+    def y_copy(k, d):
+        ref = wref(k, shard((z + NZ - d) % NZ, y), third * x, 2 * third)
+        return remote(ref, ref, sy.at[k, d], ry.at[k, d], device(x, z, 1 - y, c))
+
+    def y_wait(k, d):
+        ref = wref(k, shard((z + NZ - d) % NZ, 1 - y), third * x, 2 * third)
+        remote(ref, ref, sy.at[k, d], ry.at[k, d], device(x, z, 1 - y, c)).wait_recv()
+
+    def x_copy(k, d, e):
+        ref = wref(k, shard((z + NZ - d) % NZ, (y + e) % 2), 2 * third * x, third)
+        return remote(ref, ref, sx.at[k, 2 * d + e], rx.at[k, 2 * d + e], device(1 - x, z, y, c))
+
+    def x_wait(k, d, e):
+        ref = wref(k, shard((z + NZ - d) % NZ, (y + e) % 2), 2 * third * (1 - x), third)
+        remote(ref, ref, sx.at[k, 2 * d + e], rx.at[k, 2 * d + e], device(1 - x, z, y, c)).wait_recv()
+
+    def c_copy(k, d, e):
+        ref = wref(k, shard((z + NZ - d) % NZ, (y + e) % 2), 0, R)
+        return remote(ref, ref, sc.at[k, 2 * d + e], rc.at[k, 2 * d + e], device(x, z, y, 1 - c))
+
+    def c_wait(k, d, e):
+        other = ((z + NZ - d) % NZ) * 4 + ((y + e) % 2) * 2 + 1 - c
+        ref = wref(k, other, 0, R)
+        remote(ref, ref, sc.at[k, 2 * d + e], rc.at[k, 2 * d + e], device(x, z, y, 1 - c)).wait_recv()
+
+    for k in range(16):
+        local[k].wait()
+        for d in range(1, NZ):
+            z_copy(k, d).start()
+        y_copy(k, 0).start()
+        c_copy(k, 0, 0).start()
+
+    def gather_step(t):
+        @pl.when(t < 16)
+        def _():
+            for d in range(1, NZ):
+                z_wait(t, d)
+                y_copy(t, d).start()
+                x_copy(t, d, 0).start()
+
+        @pl.when((t >= 1) & (t < 17))
+        def _():
+            for d in range(NZ):
+                y_wait(t - 1, d)
+                x_copy(t - 1, d, 1).start()
+
+        @pl.when((t >= 2) & (t < 18))
+        def _():
+            for e in range(2):
+                for d in range(NZ):
+                    if d or e:
+                        x_wait(t - 2, d, e)
+                        c_copy(t - 2, d, e).start()
+
+        @pl.when(t >= 3)
+        def _():
+            for e in range(2):
+                for d in range(NZ):
+                    c_wait(t - 3, d, e)
+
+    def gather_steps(lo, hi):
+        def step(t, carry):
+            gather_step(t)
+            return carry
+
+        lax.fori_loop(lo, hi, step, 0)
+
+    la, lva = g.la, g.lva
+
+    def assemble(dst, parts):
+        ta, va, tb, vb = parts
+        dst[0:la] = ta[0].astype(F32)
+        dst[la : la + g.lb] = tb[0].astype(F32)
+        if T0 > la + g.lb:
+            dst[la + g.lb : T0] = jnp.zeros((T0 - la - g.lb, D), F32)
+        dst[T0 : T0 + lva] = va[0].astype(F32)
+        dst[T0 + lva : T0 + lva + g.lvb] = vb[0].astype(F32)
+        if T1 > lva + g.lvb:
+            dst[T0 + lva + g.lvb : T] = jnp.zeros((T1 - lva - g.lvb, D), F32)
+
+    assemble(HID, rows_in)
+    S[X] = HID[...].astype(BF)
+    assemble(DR, cots_in)
+
+    def live(index, s):
+        first, second = (la, g.lb) if s == 0 else (lva, g.lvb)
+        na, nb = lens[s][0], lens[2 + s][0]
+        return ((index < first) & (index < na)) | (
+            (index >= first) & (index - first < nb) & (index - first < second)
+        )
+
+    def key_mask(qs, ks):
+        shape = (size[qs], size[ks])
+        qi = lax.broadcasted_iota(jnp.int32, shape, 0)
+        ki = lax.broadcasted_iota(jnp.int32, shape, 1)
+        q_first = la if qs == 0 else lva
+        k_first = la if ks == 0 else lva
+        same = ((qi < q_first) & (ki < k_first)) | ((qi >= q_first) & (ki >= k_first))
+        return same & live(ki, ks)
+
+    UA = (0, 1, 2, 4, 5, 6)
+    UB = (3, 7)
+
+    def wtile(s, u, i):
+        return W[s, u, :, cols(i, 256)]
+
+    def wrows(s, u, i):
+        return W[s, u, cols(i, 256), :]
+
+    NT = D // 256
+
+    def cross_project():
+        for s in (0, 1):
+            own, other = span[s], span[1 - s]
+
+            def q_tile(i):
+                CQ[0, own, cols(i, 256)] = dot(S[X, own], wtile(s, UA[0], i)).astype(BF)
+
+            loop(NT, q_tile)
+
+            def kv_tile(i):
+                m = 1 + i // NT
+                j = i % NT
+                CQ[m, other, cols(j, 256)] = dot(S[X, other], wtile(s, m, j)).astype(BF)
+
+            loop(2 * NT, kv_tile)
+
+    def self_project():
+        for s in (0, 1):
+            own = span[s]
+
+            def tile(i):
+                m = i // NT
+                j = i % NT
+                SQ[m, own, cols(j, 256)] = dot(S[H1, own], wtile(s, 4 + m, j)).astype(BF)
+
+            loop(3 * NT, tile)
+
+    def attend(src, s, ks, p_ref, o_index):
+        own, keys = span[s], span[ks]
+
+        def pair(p):
+            lanes = cols(p, 128)
+            mask = key_mask(s, ks)
+            q, k, v = src[0, own, lanes], src[1, keys, lanes], src[2, keys, lanes]
+            low = lax.broadcasted_iota(jnp.int32, q.shape, 1) < 64
+            high = lax.broadcasted_iota(jnp.int32, q.shape, 1) >= 64
+            mixed = []
+            for half in range(2):
+                qh = jnp.where(low if half == 0 else high, q, jnp.zeros_like(q))
+                scores = jnp.where(mask, dot_rt(qh, k) * 0.125, NEG)
+                top = jnp.max(scores, axis=-1, keepdims=True)
+                expon = jnp.exp(scores - top)
+                probs = expon / jnp.sum(expon, axis=-1, keepdims=True)
+                p_ref[2 * p + half] = probs
+                mixed.append(dot(probs.astype(BF), v))
+            S[o_index, own, lanes] = jnp.where(low, mixed[0], mixed[1]).astype(BF)
+
+        loop(HEADS // 2, pair)
+
+    def attend_back(src, s, ks, p_ref, gq, gk, gv):
+        own, keys = span[s], span[ks]
+
+        def pair(p):
+            lanes = cols(p, 128)
+            q, k, v = src[0, own, lanes], src[1, keys, lanes], src[2, keys, lanes]
+            do = DO[own, lanes]
+            low_q = lax.broadcasted_iota(jnp.int32, q.shape, 1) < 64
+            high_q = lax.broadcasted_iota(jnp.int32, q.shape, 1) >= 64
+            low_k = lax.broadcasted_iota(jnp.int32, k.shape, 1) < 64
+            dq, dk, dv = [], [], []
+            for half in range(2):
+                doh = jnp.where(low_q if half == 0 else high_q, do, jnp.zeros_like(do))
+                probs = p_ref[2 * p + half]
+                dp = dot_rt(doh, v)
+                ds = (probs * (dp - jnp.sum(dp * probs, axis=-1, keepdims=True))).astype(BF)
+                dq.append(dot(ds, k))
+                dk.append(dot_lt(ds, q))
+                dv.append(dot_lt(probs.astype(BF), do))
+            S[gq, own, lanes] = (jnp.where(low_q, dq[0], dq[1]) * 0.125).astype(BF)
+            S[gk, keys, lanes] = (jnp.where(low_k, dk[0], dk[1]) * 0.125).astype(BF)
+            S[gv, keys, lanes] = jnp.where(low_k, dv[0], dv[1]).astype(BF)
+
+        loop(HEADS // 2, pair)
+
+    def out_project(o_index, which):
+        for s in (0, 1):
+            own = span[s]
+
+            def tile(i):
+                RES[own, cols(i, 256)] = HID[own, cols(i, 256)] + dot(
+                    S[o_index, own], wtile(s, UB[which], i)
+                )
+
+            loop(NT, tile)
+
+    RB = 16
+    NB0 = T0 // RB
+    mean = lambda v: jnp.sum(v, axis=-1, keepdims=True) * (1.0 / D)
+
+    def normalize(i, r):
+        resid = RES[r]
+        centre = resid - mean(resid)
+        rstd = lax.rsqrt(mean(centre * centre) + 1e-05)
+        return centre * rstd, rstd
+
+    def row_of(i, s):
+        return vecs[pl.ds(s * 3 + i, 1), :]
+
+    def norm_forward(i, h_index):
+        def block(b):
+            s = b // NB0
+            r = cols(b, RB)
+            xh, rstd = normalize(i, r)
+            XH[i, r] = xh
+            RSTD[i, r] = rstd
+            hidden = xh * vecs[pl.ds(s * 3 + i, 1), :] + vecs[pl.ds(6 + s * 3 + i, 1), :]
+            HID[r] = hidden
+            S[h_index, r] = hidden.astype(BF)
+
+        loop(T // RB, block)
+
+    def add_row(row, value):
+        VG[pl.ds(row, 1), :] += jnp.sum(value, axis=0, keepdims=True)
+
+    def norm_pull(i, s, r, dh, xh, rstd):
+        add_row(s * 3 + i, dh * xh)
+        add_row(6 + s * 3 + i, dh)
+        dx = dh * vecs[pl.ds(s * 3 + i, 1), :]
+        return rstd * (dx - mean(dx) - xh * mean(dx * xh))
+
+    def norm_backward(i, g_index):
+        def block(b):
+            s = b // NB0
+            r = cols(b, RB)
+            dr = norm_pull(i, s, r, DR[r], XH[i, r], RSTD[i, r])
+            DR[r] = dr
+            S[g_index, r] = dr.astype(BF)
+
+        loop(T // RB, block)
+
+    def tail():
+        def block(b):
+            s = b // NB0
+            r = cols(b, RB)
+            xh, rstd = normalize(2, r)
+            gain = vecs[pl.ds(s * 3 + 2, 1), :]
+            h3 = xh * gain + vecs[pl.ds(6 + s * 3 + 2, 1), :]
+            gate = vecs[pl.ds(12 + s, 1), :]
+            logit = jnp.sum(h3 * gate, axis=-1, keepdims=True)
+            sig = 1.0 / (1.0 + jnp.exp(-logit))
+            index = lax.broadcasted_iota(jnp.int32, (RB, 1), 0) + b * RB
+            text = index < T0
+            mask = (text & live(index, 0)) | ((index >= T0) & live(index - T0, 1))
+            mask = jnp.where(mask, 1.0, 0.0)
+            weight = sig * mask
+            HID[r] = h3 * weight
+            dout = DR[r]
+            dlogit = jnp.sum(dout * h3, axis=-1, keepdims=True) * weight * (1.0 - sig)
+            add_row(12 + s, h3 * dlogit)
+            dr = norm_pull(2, s, r, dout * weight + dlogit * gate, xh, rstd)
+            DR[r] = dr
+            S[DF, r] = dr.astype(BF)
+
+        loop(T // RB, block)
+        o_ta, o_va, o_tb, o_vb = outs
+        o_ta[0] = HID[0:la].astype(BF)
+        o_tb[0] = HID[la : la + g.lb].astype(BF)
+        o_va[0] = HID[T0 : T0 + lva].astype(BF)
+        o_vb[0] = HID[T0 + lva : T0 + lva + g.lvb].astype(BF)
+
+    def ffn_up(q):
+        for s in (0, 1):
+            own = span[s]
+
+            def tile(i):
+                j = q * NT + i
+                u = dot(S[H2, own], wtile(s, 8 + q, i))
+                cdf = 0.5 + 0.5 * erf_of(u * 0.7071067811865476)
+                A[own, cols(j, 256)] = (u * cdf).astype(BF)
+                GP[own, cols(j, 256)] = cdf + u * (
+                    jnp.exp(u * u * -0.5) * 0.3989422804014327
+                )
+
+            loop(NT, tile)
+
+    def ffn_down():
+        for s in (0, 1):
+            own = span[s]
+
+            def tile(i):
+                total = HID[own, cols(i, 256)]
+                for q in range(4):
+                    total = total + dot(A[own, D * q : D * q + D], wtile(s, 12 + q, i))
+                RES[own, cols(i, 256)] = total
+
+            loop(NT, tile)
+
+    def ffn_down_back():
+        for s in (0, 1):
+            own = span[s]
+
+            def tile(j):
+                da = dot_rt(S[DF, own], wrows(s, 12 + j // NT, j % NT))
+                DU[own, cols(j, 256)] = (GP[own, cols(j, 256)] * da).astype(BF)
+
+            loop(4 * NT, tile)
+
+    def ffn_up_back():
+        for s in (0, 1):
+            own = span[s]
+
+            def tile(i):
+                total = DR[own, cols(i, 256)]
+                for q in range(4):
+                    total = total + dot_rt(DU[own, D * q : D * q + D], wrows(s, 8 + q, i))
+                DR[own, cols(i, 256)] = total
+
+            loop(NT, tile)
+
+    def out_back(g_index, which):
+        for s in (0, 1):
+            own = span[s]
+
+            def tile(i):
+                DO[own, cols(i, 256)] = dot_rt(
+                    S[g_index, own], wrows(s, UB[which], i)
+                ).astype(BF)
+
+            loop(NT, tile)
+
+    def self_back():
+        for s in (0, 1):
+            own = span[s]
+
+            def tile(i):
+                total = DR[own, cols(i, 256)]
+                for m, gi in enumerate((DQS, DKS, DVS)):
+                    total = total + dot_rt(S[gi, own], wrows(s, 4 + m, i))
+                DR[own, cols(i, 256)] = total
+
+            loop(NT, tile)
+
+    def cross_back():
+        for s in (0, 1):
+            own = span[s]
+
+            def tile(i):
+                total = DR[own, cols(i, 256)] + dot_rt(S[DQC, own], wrows(s, 0, i))
+                total = total + dot_rt(S[DKC, own], wrows(1 - s, 1, i))
+                total = total + dot_rt(S[DVC, own], wrows(1 - s, 2, i))
+                DR[own, cols(i, 256)] = total
+
+            loop(NT, tile)
+        g_ta, g_va, g_tb, g_vb = grads
+        g_ta[0] = DR[0:la].astype(BF)
+        g_tb[0] = DR[la : la + g.lb].astype(BF)
+        g_va[0] = DR[T0 : T0 + lva].astype(BF)
+        g_vb[0] = DR[T0 + lva : T0 + lva + g.lvb].astype(BF)
+
+    sends = []
+
+    def plane_send(r, src, dst, slot):
+        @pl.when(me != r)
+        def _():
+            remote(src, dst, s_ex.at[slot, r], r_ex.at[slot, me], role_device(r)).start()
+
+        @pl.when(me == r)
+        def _():
+            pltpu.make_async_copy(src, dst, s_own.at[slot]).start()
+
+        sends.append((r, src, dst, slot))
+
+    def finish_sends():
+        for r, src, dst, slot in sends:
+
+            @pl.when(me != r)
+            def _():
+                remote(src, dst, s_ex.at[slot, r], r_ex.at[slot, me], role_device(r)).wait_send()
+
+    def plane_wait(slot, pick):
+        for p in range(8):
+            ref = pick(p)
+
+            @pl.when(me != p)
+            def _():
+                remote(ref, ref, s_ex.at[slot, p], r_ex.at[slot, p], role_device(p)).wait_recv()
+
+            @pl.when(me == p)
+            def _():
+                pltpu.make_async_copy(ref, ref, s_own.at[slot]).wait()
+
+    A_OF = (X, X, X, H1, H1, H1, OC, OS)
+    G_OF = (DQC, DKC, DVC, DQS, DKS, DVS, DC, DS)
+    HB = D // 2
+
+    def send_left(r):
+        plane_send(r, S.at[A_OF[r]], ra.at[me], 0)
+
+    def send_right(r):
+        plane_send(r, S.at[G_OF[r]], rg.at[me], 1)
+
+    def send_ffn_left(r):
+        if r < 4:
+            plane_send(r, S.at[H2], rfa.at[me, :, pl.ds(0, D)], 3)
+        else:
+            yy = (r - 4) // 2
+            for q in range(4):
+                plane_send(
+                    r, A.at[:, pl.ds(D * q + HB * yy, HB)], rfa.at[me, :, pl.ds(HB * q, HB)],
+                    3 + q,
+                )
+
+    def send_ffn_right(r):
+        if r < 4:
+            plane_send(r, DU.at[:, pl.ds(D * r, D)], rfg.at[me], 2)
+        else:
+            hh = (r - 4) % 2
+            plane_send(r, S.at[DF, :, pl.ds(HB * hh, HB)], rfg.at[me, :, pl.ds(0, HB)], 2)
+
+    st = [0]
+
+    def stage(src, dst_unit, col, width, dcol):
+        copies = []
+        for half in range(2):
+            for p in range(4):
+                cp = pltpu.make_async_copy(
+                    src.at[4 * half + p, :, pl.ds(col, width)],
+                    W.at[half, dst_unit, pl.ds(T * p, T), pl.ds(dcol, width)],
+                    s_st.at[st[0]],
+                )
+                st[0] += 1
+                cp.start()
+                copies.append(cp)
+        return copies
+
+    def stacked(unit, rs, lanes):
+        first, count = (0, T0) if rs == 0 else (T0, T1)
+        return jnp.concatenate(
+            [
+                W[half, unit, T * p + first : T * p + first + count, lanes]
+                for half in range(2)
+                for p in range(4)
+            ],
+            axis=0,
+        )
+
+    def weight_grad(left, right, dst):
+        for rs in range(2):
+
+            def tile(i):
+                W[rs, dst, cols(i, 256), :] = dot_lt(
+                    stacked(left, rs, cols(i, 256)), stacked(right, rs, slice(0, D))
+                ).astype(BF)
+
+            loop(NT, tile)
+
+    def weight_grad_down(right, dst):
+        for rs in range(2):
+
+            def tile(q):
+                left_unit = 10 + q // 2
+                out = dot_lt(
+                    stacked(left_unit, rs, cols(q % 2, HB)), stacked(right, rs, slice(0, HB))
+                ).astype(BF)
+                W[rs, dst, pl.ds(pl.multiple_of(q * ZR, ZR), ZR), 0:HB] = out[0:ZR]
+                W[rs, dst, pl.ds(pl.multiple_of(q * ZR, ZR), ZR), HB:D] = out[ZR : 2 * ZR]
+
+            loop(4, tile)
+
+    def z_send(n, unit, d):
+        zz = (z + d) % NZ
+        src = W.at[:, unit, pl.ds(pl.multiple_of(zz * ZR, ZR), ZR)]
+        return remote(src, RZ.at[n, d - 1], s_zr.at[n, d - 1], r_zr.at[n, d - 1], device(x, zz, y, c))
+
+    def z_collect(n, unit):
+        for d in range(1, NZ):
+            z_send(n, unit, d).wait_recv()
+        for rs in range(2):
+
+            def block(i):
+                total = W[rs, unit, pl.ds(pl.multiple_of(z * ZR + i * 16, 16), 16)].astype(F32)
+                for d in range(NZ - 1):
+                    total = total + RZ[n, d, rs, cols(i, 16)].astype(F32)
+                FB[n, rs, cols(i, 16)] = total.astype(BF)
+
+            loop(ZR // 16, block)
+
+    flip = (((me + 1) // 2) % 2) * (1 - (me // 3 + 1) // 2)
+
+    def attn_blocks(r):
+        yy, cc = (r // 2) % 2, r % 2
+        for rs in range(2):
+            src = FB.at[0, rs, pl.ds(R * (2 * yy + cc), R)]
+            s = rs + flip - 2 * rs * flip
+            yield rs, src, ga.at[s, me]
+
+    def up_blocks(r):
+        yy, cc = (r // 2) % 2, r % 2
+        for rs in range(2):
+            src = FB.at[1, rs, pl.ds(R * (2 * yy + cc), R)]
+            yield 2 + rs, src, gu.at[rs, :, pl.ds(pl.multiple_of(D * (me % 4), 128), D)]
+
+    def down_blocks(r):
+        cc = r % 2
+        for rs in range(2):
+            src = FB.at[1, rs, :, pl.ds(HB * cc, HB)]
+            yield 2 + rs, src, gd.at[rs, :, pl.ds(pl.multiple_of(HB * (me % 2), 128), HB)]
+
+    def spread(r, blocks, cond, act):
+        for n, src, dst in blocks(r):
+
+            @pl.when(cond & (me != r))
+            def _():
+                cp = remote(src, dst, s_rd.at[n, r], r_rd.at[n, me], role_device(r))
+                cp.start() if act == "start" else cp.wait_send()
+
+            @pl.when(cond & (me == r))
+            def _():
+                cp = pltpu.make_async_copy(src, dst, s_own.at[8 + n])
+                cp.start() if act == "start" else cp.wait()
+
+    def spread_all(n, act):
+        for r in range(8):
+            if n == 0:
+                spread(r, attn_blocks, me >= 0, act)
+            else:
+                spread(r, up_blocks, me < 4, act)
+                spread(r, down_blocks, (me // 2 == 2 + (r // 2) % 2), act)
+
+    def spread_wait():
+        for p in range(8):
+
+            @pl.when(me != p)
+            def _():
+                for rs in range(2):
+                    ref = ga.at[rs, p]
+                    remote(ref, ref, s_rd.at[rs, p], r_rd.at[rs, p], role_device(p)).wait_recv()
+                    if p < 4:
+                        ref = gu.at[rs, :, pl.ds(D * p, D)]
+                        remote(
+                            ref, ref, s_rd.at[2 + rs, p], r_rd.at[2 + rs, p], role_device(p)
+                        ).wait_recv()
+
+            if p >= 4:
+
+                @pl.when((me != p) & (y == (p - 4) // 2))
+                def _():
+                    for rs in range(2):
+                        ref = gd.at[rs, :, pl.ds(HB * (p % 2), HB)]
+                        remote(
+                            ref, ref, s_rd.at[2 + rs, p], r_rd.at[2 + rs, p], role_device(p)
+                        ).wait_recv()
+
+    VG[...] = jnp.zeros_like(VG)
+    for step in range(1, g.fsdp):
+        vec_wait(step)
+    own_vec.wait()
+    total = jnp.zeros((16, D), F32)
+    lane = lax.broadcasted_iota(jnp.int32, (128, D), 0)
+    col = lax.broadcasted_iota(jnp.int32, (128, D), 1)
+    for ff in range(g.fsdp):
+        pick = ((col == lane + R * ff) & (lane < R)).astype(F32).astype(BF)
+        total = total + dot(VEC[ff], pick)
+    vecs[...] = total
+
+    gather_steps(0, 7)
+    cross_project()
+    gather_steps(7, 8)
+    attend(CQ, 0, 1, p_refs[0], OC)
+    attend(CQ, 1, 0, p_refs[1], OC)
+    gather_steps(8, 9)
+    out_project(OC, 0)
+    norm_forward(0, H1)
+    gather_steps(9, 11)
+    self_project()
+    gather_steps(11, 12)
+    attend(SQ, 0, 0, p_refs[2], OS)
+    attend(SQ, 1, 1, p_refs[3], OS)
+    gather_steps(12, 13)
+    out_project(OS, 1)
+    norm_forward(1, H2)
+    gather_steps(13, 15)
+    for q in range(4):
+        gather_steps(15 + q, 16 + q)
+        ffn_up(q)
+
+    def gather_sent(k):
+        for d in range(1, NZ):
+            z_copy(k, d).wait_send()
+        for d in range(NZ):
+            y_copy(k, d).wait_send()
+            for e in range(2):
+                c_copy(k, d, e).wait_send()
+                if d or e:
+                    x_copy(k, d, e).wait_send()
+
+    loop(16, gather_sent)
+    for r in range(8):
+        send_ffn_left(r)
+    for r in range(8):
+        send_left(r)
+    ffn_down()
+    tail()
+    for r in range(4, 8):
+        send_ffn_right(r)
+    ffn_down_back()
+    for r in range(4):
+        send_ffn_right(r)
+    ffn_up_back()
+    norm_backward(1, DS)
+    send_right(7)
+    out_back(DS, 1)
+    attend_back(SQ, 0, 0, p_refs[2], DQS, DKS, DVS)
+    attend_back(SQ, 1, 1, p_refs[3], DQS, DKS, DVS)
+    for r in (3, 4, 5):
+        send_right(r)
+    self_back()
+    norm_backward(0, DC)
+    send_right(6)
+    out_back(DC, 0)
+    attend_back(CQ, 0, 1, p_refs[0], DQC, DKC, DVC)
+    attend_back(CQ, 1, 0, p_refs[1], DQC, DKC, DVC)
+    for r in (0, 1, 2):
+        send_right(r)
+
+    def vg_copy(r):
+        return remote(VG, VR.at[me], s_vg.at[r], r_vg.at[me], role_device(r))
+
+    for r in range(8):
+
+        @pl.when(me != r)
+        def _():
+            vg_copy(r).start()
+
+    VR[me] = VG[...]
+    cross_back()
+
+    @pl.when(me < 4)
+    def _():
+        plane_wait(2, lambda p: rfg.at[p])
+        plane_wait(3, lambda p: rfa.at[p, :, pl.ds(0, D)])
+
+    @pl.when(me >= 4)
+    def _():
+        plane_wait(2, lambda p: rfg.at[p, :, pl.ds(0, HB)])
+        for q in range(4):
+            plane_wait(3 + q, lambda p: rfa.at[p, :, pl.ds(HB * q, HB)])
+
+    copies = stage(rfg, 12, 0, D, 0) + stage(rfa, 10, 0, D, 0) + stage(rfa, 11, D, D, 0)
+    for cp in copies:
+        cp.wait()
+
+    @pl.when(me < 4)
+    def _():
+        weight_grad(10, 12, 15)
+
+    @pl.when(me >= 4)
+    def _():
+        weight_grad_down(12, 15)
+
+    for d in range(1, NZ):
+        z_send(1, 15, d).start()
+
+    plane_wait(0, lambda p: ra.at[p])
+    plane_wait(1, lambda p: rg.at[p])
+    copies = stage(ra, 8, 0, D, 0) + stage(rg, 9, 0, D, 0)
+    for cp in copies:
+        cp.wait()
+    weight_grad(8, 9, 14)
+    for d in range(1, NZ):
+        z_send(0, 14, d).start()
+
+    for p in range(8):
+
+        @pl.when(me != p)
+        def _():
+            ref = VR.at[p]
+            remote(ref, ref, s_vg.at[p], r_vg.at[p], role_device(p)).wait_recv()
+
+    total = VR[0]
+    for p in range(1, 8):
+        total = total + VR[p]
+    VZ[z] = total
+
+    def vz_copy(d):
+        return remote(
+            VZ.at[z], VZ.at[z], s_vz.at[d - 1], r_vz.at[d - 1], device(x, (z + d) % NZ, y, c)
+        )
+
+    for d in range(1, NZ):
+        vz_copy(d).start()
+    z_collect(1, 15)
+    spread_all(1, "start")
+    for d in range(1, NZ):
+        ref = VZ.at[(z + NZ - d) % NZ]
+        remote(ref, ref, s_vz.at[d - 1], r_vz.at[d - 1], device(x, z, y, c)).wait_recv()
+    total = VZ[0]
+    for zz in range(1, NZ):
+        total = total + VZ[zz]
+    vec_out[...] = total
+    z_collect(0, 14)
+    spread_all(0, "start")
+
+    for step in range(1, g.fsdp):
+        vec_copy(step).wait_send()
+    finish_sends()
+    for r in range(8):
+
+        @pl.when(me != r)
+        def _():
+            vg_copy(r).wait_send()
+
+    for d in range(1, NZ):
+        vz_copy(d).wait_send()
+        z_send(0, 14, d).wait_send()
+        z_send(1, 15, d).wait_send()
+    spread_wait()
+    spread_all(1, "wait")
+    spread_all(0, "wait")
+
+
+def kernel_path(g, *args):
+    rows, lens, cots = args[0:4], args[4:8], args[8:12]
+    weights = args[12:16]
+    gain, bias, gate = args[16:19]
+    D, FF, R, T, T0, T1, NZ = g.d, g.ff, g.rows, g.t, g.t0, g.t1, g.nz
+    vec = jnp.concatenate([gain.reshape(6, R), bias.reshape(6, R), gate], axis=0)
+    vec = jnp.pad(vec, ((0, 2), (0, 128 - R)))
+    vmem = lambda *shape: pltpu.VMEM(shape[:-1], shape[-1])
+    dma = lambda *shape: pltpu.SemaphoreType.DMA(shape)
+    in_vmem = pl.BlockSpec(memory_space=pltpu.VMEM)
+    in_any = pl.BlockSpec(memory_space=pl.ANY)
+    in_smem = pl.BlockSpec(memory_space=pltpu.SMEM)
+    row_shapes = [jax.ShapeDtypeStruct(r.shape, BF) for r in rows]
+    out_shape = row_shapes * 2 + [
+        jax.ShapeDtypeStruct((2, 8, R, D), BF),
+        jax.ShapeDtypeStruct((2, R, FF), BF),
+        jax.ShapeDtypeStruct((2, 4 * R, D), BF),
+        jax.ShapeDtypeStruct((16, D), F32),
+        jax.ShapeDtypeStruct((8, T, D), BF),
+        jax.ShapeDtypeStruct((8, T, D), BF),
+        jax.ShapeDtypeStruct((8, T, 2 * D), BF),
+        jax.ShapeDtypeStruct((8, T, D), BF),
+    ]
+    scratch = [
+        vmem(2, 16, D, D, BF),
+        vmem(g.fsdp, 16, 128, BF),
+        vmem(16, D, F32),
+        vmem(14, T, D, BF),
+        vmem(T, FF, BF),
+        vmem(T, FF, BF),
+        vmem(3, T, D, BF),
+        vmem(3, T, D, BF),
+        vmem(T, D, BF),
+        vmem(T, D, F32),
+        vmem(T, D, F32),
+        vmem(T, D, F32),
+        vmem(3, T, D, F32),
+        vmem(3, T, 1, F32),
+        vmem(T, FF, F32),
+        vmem(HEADS, T0, T1, F32),
+        vmem(HEADS, T1, T0, F32),
+        vmem(HEADS, T0, T0, F32),
+        vmem(HEADS, T1, T1, F32),
+        vmem(2, NZ - 1, 2, D // NZ, D, BF),
+        vmem(2, 2, D // NZ, D, BF),
+        vmem(16, D, F32),
+        vmem(8, 16, D, F32),
+        vmem(NZ, 16, D, F32),
+        dma(17),
+        dma(g.fsdp - 1),
+        dma(g.fsdp - 1),
+        dma(16, NZ - 1),
+        dma(16, NZ - 1),
+        dma(16, NZ),
+        dma(16, NZ),
+        dma(16, 2 * NZ),
+        dma(16, 2 * NZ),
+        dma(16, 2 * NZ),
+        dma(16, 2 * NZ),
+        dma(7, 8),
+        dma(7, 8),
+        dma(12),
+        dma(40),
+        dma(2, NZ - 1),
+        dma(2, NZ - 1),
+        dma(4, 8),
+        dma(4, 8),
+        dma(8),
+        dma(8),
+        dma(NZ - 1),
+        dma(NZ - 1),
+    ]
+    results = pl.pallas_call(
+        partial(layer_kernel, g),
+        out_shape=out_shape,
+        in_specs=[in_smem] * 4 + [in_vmem] * 8 + [in_any] * 5,
+        out_specs=[in_vmem] * 8 + [in_any] * 3 + [in_vmem] + [in_any] * 4,
+        scratch_shapes=scratch,
+        compiler_params=pltpu.CompilerParams(
+            collective_id=0, has_side_effects=True, vmem_limit_bytes=67043328
+        ),
+        name="layer",
+    )(*lens, *rows, *cots, *weights, vec)
+    ga, gu, gd, vectors = results[8:12]
+    ga = ga.astype(F32)
+    own = lax.dynamic_slice(vectors, (0, lax.axis_index("fsdp") * R), (16, R))
+    return (
+        *results[:8],
+        ga[:, :6],
+        ga[:, 6:],
+        gu.astype(F32),
+        gd.astype(F32),
+        own[0:6].reshape(2, 3, R),
+        own[6:12].reshape(2, 3, R),
+        own[12:14],
+    )
+
+
 def solution(mesh):
+    def per_device(*args):
+        g = Geometry(mesh, [a.shape for a in args])
+        return kernel_path(g, *args) if g.fits() else plain_path(*args)
+
     in_specs = (
         P(("dp", "fsdp"), None, None),
         P(("dp", "fsdp"), None, None),

time: 1650 us -> 422 us (0.26)
  waiting for transfers between devices: 1000 us -> 0 us
  Pallas kernels: 0 us -> 395 us
  matrix products: 268 us -> 0 us
  blocking collectives: 143 us -> 0 us
  other arithmetic: 93.7 us -> 3.46 us
  local copies, waits for them, and re-layouts: 96.1 us -> 13.3 us
  between operations: 22.9 us -> 3.32 us
    reduce_scatter x4 -> x0, waiting for transfers between devices: 786 us -> none  [the longest x1 258 us: per_device(): lax.psum_scatter(packed[0], ('dp', 'fsdp'), scatter_dimension=1, tiled=True)]
    pallas_call x0 -> x1, Pallas kernels: none -> 395 us  [kernel_path(): pl.pallas_call(partial(layer_kernel, g), out_shape=out_shape, in_specs=[i...]
    dot_general x176 -> x0, matrix products: 268 us -> none  [the longest x40 85.9 us: project_back(): jnp.einsum('ple,de->pld', grads, matrix, preferred_element_type=jnp.float32)]
    all_gather x4 -> x0, waiting for transfers between devices: 215 us -> none  [the longest x1 78.3 us: per_device(): lax.all_gather(ffn_down, 'fsdp', axis=1, tiled=True)]
    all_gather x9 -> x0, blocking collectives: 100 us -> none  [the longest x1 22.4 us: per_device(): lax.all_gather(norm_gain, 'fsdp', axis=2, tiled=True)]
    unnamed x2 -> x0, blocking collectives: 42.7 us -> none
    convert_element_type x68 -> x0, local copies, waits for them, and re-layouts: 32.5 us -> none  [the longest x16 11.6 us: attend_backward(): grad_value.reshape(value_rows.shape).astype(jnp.bfloat16)]
    concatenate x7 -> x1, other arithmetic: 31.6 us -> 1.26 us  [kernel_path(): jnp.concatenate([gain.reshape(6, R), bias.reshape(6, R), gate], axis=0)]
  transfers between devices with their start and end apart: 10 -> 0, of which waited for: 8 -> 0; matrix products, arithmetic and copies ran while one was open for 13% -> 0% of each run, Pallas kernels for 0% -> 0%
where the time goes in v2:
time: 422 us; the launch traced here: 415 us
  Pallas kernels  395 us (94%)
  local copies, waits for them, and re-layouts  13.3 us (3%)
    pallas_call x1, Pallas kernels, kernel_path(): pl.pallas_call(partial(layer_kernel, g), out_shape=out_shape, in_specs=[i...  395 us

profile of v2, /device:TPU:31, one launch (start us, length us, event | category | flops | bytes accessed | tf_op | source)
XLA Modules:
  0.0 415.0 jit_solution(3102364594078804425)
XLA Ops:
  0.6 0.7 copy.38
  1.3 0.7 copy.39
  2.1 1.3 fusion.8.refs_16_
  5.9 394.9 %layer.1 = (bf16[1,48,768]{2,1,0:T(8,128)(2,1)}, bf16[1,20,768]{2,1,0:T(8,128)(2,1)}, bf16[1,56,768]{2,1,0:T(8,128)(2,1)}, bf16[1,28,768]{2,1,0:T(8,128)(2,1)}, ...) custom-call(s32[1]{0:T(128)S(6)} %copy.50.refs_0_, ...), custom_call_target="tpu_custom_call" | custom-call | tf_op jit(solution)/shard_map/layer/pallas_call | solution.py:1376
  400.8 0.0 copy-start
  400.8 0.9 fusion.9
  401.7 0.6 copy.40
  402.3 0.6 copy.41
  402.9 1.3 dynamic-slice.2
  404.2 0.0 copy-start.2
  404.2 2.6 slice.20
  406.8 0.0 copy-done
  406.8 0.0 copy-start.1
  406.8 0.9 slice.21
  407.7 0.0 copy-start.6
  407.7 0.0 copy-start.10
  407.7 0.0 copy-start.4
  407.7 0.0 copy-done.2
  407.7 0.0 copy-start.8
  407.7 0.0 copy-start.5
  407.7 0.0 copy-start.9
  407.7 0.0 copy-start.3
  407.7 0.0 copy-start.7
  407.7 1.1 convert_element_type.12
  408.8 0.0 copy-done.1
  408.8 1.1 convert_element_type.13
  409.9 0.0 copy-done.6
  409.9 0.6 copy.54
  410.6 0.0 copy-done.10
  410.6 0.6 copy.55
  411.2 0.0 copy-done.4
  411.2 0.6 copy.56
  411.8 0.0 copy-done.8
  411.8 0.6 copy.57
  412.5 0.0 copy-done.5
  412.5 0.6 copy.58
  413.1 0.0 copy-done.9
  413.1 0.6 copy.59
  413.7 0.0 copy-done.3
  413.7 0.6 copy.60
  414.4 0.0 copy-done.7
  414.4 0.6 copy.61
  (4 shorter events, 0.1 us)
Async XLA Ops:
  400.8 6.0 %copy-start = (bf16[2,8,48,768]{3,2,1,0:T(8,128)(2,1)S(1)}, bf16[2,8,48,768]{3,2,1,0:T(8,128)(2,1)}, u32[]{:S(2)}) copy-start(bf16[2,8,48,768]{3,2,1,0:T(8,128)(2,1)} %get-tuple-element.35) | copy-start | bytes 3538948
  404.2 3.5 copy-start.2
  406.8 2.0 copy-start.1
  407.7 2.3 copy-start.6
  407.7 2.9 copy-start.10
  407.7 3.5 copy-start.4
  407.7 4.2 %copy-start.8 = (bf16[1,28,768]{2,1,0:T(8,128)(2,1)S(1)}, bf16[1,28,768]{2,1,0:T(8,128)(2,1)}, u32[]{:S(2)}) copy-start(bf16[1,28,768]{2,1,0:T(8,128)(2,1)} %get-tuple-element.89) | copy-start | bytes 129028
  407.7 4.8 %copy-start.5 = (bf16[1,48,768]{2,1,0:T(8,128)(2,1)S(1)}, bf16[1,48,768]{2,1,0:T(8,128)(2,1)}, u32[]{:S(2)}) copy-start(bf16[1,48,768]{2,1,0:T(8,128)(2,1)} %get-tuple-element.90) | copy-start | bytes 221188
  407.7 5.4 %copy-start.9 = (bf16[1,20,768]{2,1,0:T(8,128)(2,1)S(1)}, bf16[1,20,768]{2,1,0:T(8,128)(2,1)}, u32[]{:S(2)}) copy-start(bf16[1,20,768]{2,1,0:T(8,128)(2,1)} %get-tuple-element.91) | copy-start | bytes 92164
  407.7 6.0 %copy-start.3 = (bf16[1,56,768]{2,1,0:T(8,128)(2,1)S(1)}, bf16[1,56,768]{2,1,0:T(8,128)(2,1)}, u32[]{:S(2)}) copy-start(bf16[1,56,768]{2,1,0:T(8,128)(2,1)} %get-tuple-element.92) | copy-start | bytes 258052
  407.7 6.6 %copy-start.7 = (bf16[1,28,768]{2,1,0:T(8,128)(2,1)S(1)}, bf16[1,28,768]{2,1,0:T(8,128)(2,1)}, u32[]{:S(2)}) copy-start(bf16[1,28,768]{2,1,0:T(8,128)(2,1)} %get-tuple-element.93) | copy-start | bytes 129028

commit v3 on v2

--- a/solution.py
+++ b/solution.py
@@ -505,13 +505,13 @@
     x = lax.axis_index("dp")
     f = lax.axis_index("fsdp")
     z, y, c = f // 4, (f // 2) % 2, f % 2
-    me = x * 4 + y * 2 + c
+    me = c * 4 + x * 2 + y
 
     def device(xx, zz, yy, cc):
         return (xx, zz * 4 + yy * 2 + cc)
 
     def role_device(r):
-        return device(r // 4, z, (r // 2) % 2, r % 2)
+        return device((r // 2) % 2, z, r % 2, r // 4)
 
     def remote(src, dst, send, recv, dev):
         return pltpu.make_async_remote_copy(
@@ -531,24 +531,27 @@
     pl.semaphore_wait(barrier, g.fsdp + 3)
 
     def wref(k, ff, r0, n):
-        down = k // 12
-        unit = k + down * (12 + (4 * R * ff) // D - k)
-        row = R * ff + down * ((4 * R * ff) % D + R * (k - 12) - R * ff) + r0
-        return W.at[:, unit, pl.ds(pl.multiple_of(row, 16), n)]
+        kk = k % 16
+        down = kk // 12
+        unit = kk + down * (12 + (4 * R * ff) // D - kk)
+        row = R * ff + down * ((4 * R * ff) % D + R * (kk - 12) - R * ff) + r0
+        return W.at[k // 16, unit, pl.ds(pl.multiple_of(row, 16), n)]
 
     def local_part(k):
         w_in, w_out, w_up, w_dn = w_parts
+        s, k = k // 16, k % 16
         if k in (3, 7):
-            return w_out.at[:, (k - 3) // 4]
+            return w_out.at[s, (k - 3) // 4]
         if k < 8:
-            return w_in.at[:, (0, 1, 2, None, 3, 4, 5)[k]]
+            return w_in.at[s, (0, 1, 2, None, 3, 4, 5)[k]]
         if k < 12:
-            return w_up.at[:, :, pl.ds(D * (k - 8), D)]
-        return w_dn.at[:, pl.ds(R * (k - 12), R)]
+            return w_up.at[s, :, pl.ds(D * (k - 8), D)]
+        return w_dn.at[s, pl.ds(R * (k - 12), R)]
 
     third = R // 3
+    NK = 32
     local = []
-    for k in range(16):
+    for k in range(NK):
         cp = pltpu.make_async_copy(local_part(k), wref(k, f, 0, R), s_loc.at[k])
         cp.start()
         local.append(cp)
@@ -565,7 +568,7 @@
 
     for step in range(1, g.fsdp):
         vec_copy(step).start()
-    own_vec = pltpu.make_async_copy(vec_in, VEC.at[f], s_loc.at[16])
+    own_vec = pltpu.make_async_copy(vec_in, VEC.at[f], s_loc.at[NK])
     own_vec.start()
 
     def shard(zz, yy):
@@ -604,7 +607,7 @@
         ref = wref(k, other, 0, R)
         remote(ref, ref, sc.at[k, 2 * d + e], rc.at[k, 2 * d + e], device(x, z, y, 1 - c)).wait_recv()
 
-    for k in range(16):
+    for k in range(NK):
         local[k].wait()
         for d in range(1, NZ):
             z_copy(k, d).start()
@@ -612,20 +615,20 @@
         c_copy(k, 0, 0).start()
 
     def gather_step(t):
-        @pl.when(t < 16)
+        @pl.when(t < NK)
         def _():
             for d in range(1, NZ):
                 z_wait(t, d)
                 y_copy(t, d).start()
                 x_copy(t, d, 0).start()
 
-        @pl.when((t >= 1) & (t < 17))
+        @pl.when((t >= 1) & (t < NK + 1))
         def _():
             for d in range(NZ):
                 y_wait(t - 1, d)
                 x_copy(t - 1, d, 1).start()
 
-        @pl.when((t >= 2) & (t < 18))
+        @pl.when((t >= 2) & (t < NK + 2))
         def _():
             for e in range(2):
                 for d in range(NZ):
@@ -690,40 +693,38 @@
 
     NT = D // 256
 
-    def cross_project():
-        for s in (0, 1):
-            own, other = span[s], span[1 - s]
-
-            def q_tile(i):
-                CQ[0, own, cols(i, 256)] = dot(S[X, own], wtile(s, UA[0], i)).astype(BF)
-
-            loop(NT, q_tile)
-
-            def kv_tile(i):
-                m = 1 + i // NT
-                j = i % NT
-                CQ[m, other, cols(j, 256)] = dot(S[X, other], wtile(s, m, j)).astype(BF)
-
-            loop(2 * NT, kv_tile)
-
-    def self_project():
-        for s in (0, 1):
-            own = span[s]
-
-            def tile(i):
-                m = i // NT
-                j = i % NT
-                SQ[m, own, cols(j, 256)] = dot(S[H1, own], wtile(s, 4 + m, j)).astype(BF)
-
-            loop(3 * NT, tile)
-
-    def attend(src, s, ks, p_ref, o_index):
+    def cross_project(s):
+        own, other = span[s], span[1 - s]
+
+        def q_tile(i):
+            CQ[0, own, cols(i, 256)] = dot(S[X, own], wtile(s, 0, i)).astype(BF)
+
+        loop(NT, q_tile)
+
+        def kv_tile(i):
+            m = 1 + i // NT
+            j = i % NT
+            CQ[m, other, cols(j, 256)] = dot(S[X, other], wtile(s, m, j)).astype(BF)
+
+        loop(2 * NT, kv_tile)
+
+    def self_project(s):
+        own = span[s]
+
+        def tile(i):
+            m = i // NT
+            j = i % NT
+            SQ[m, own, cols(j, 256)] = dot(S[H1, own], wtile(s, 4 + m, j)).astype(BF)
+
+        loop(3 * NT, tile)
+
+    def attend(src, base, s, ks, p_ref, o_index):
         own, keys = span[s], span[ks]
 
         def pair(p):
             lanes = cols(p, 128)
             mask = key_mask(s, ks)
-            q, k, v = src[0, own, lanes], src[1, keys, lanes], src[2, keys, lanes]
+            q, k, v = src[base, own, lanes], src[base + 1, keys, lanes], src[base + 2, keys, lanes]
             low = lax.broadcasted_iota(jnp.int32, q.shape, 1) < 64
             high = lax.broadcasted_iota(jnp.int32, q.shape, 1) >= 64
             mixed = []
@@ -739,12 +740,12 @@
 
         loop(HEADS // 2, pair)
 
-    def attend_back(src, s, ks, p_ref, gq, gk, gv):
+    def attend_back(src, base, s, ks, p_ref, gq, gk, gv):
         own, keys = span[s], span[ks]
 
         def pair(p):
             lanes = cols(p, 128)
-            q, k, v = src[0, own, lanes], src[1, keys, lanes], src[2, keys, lanes]
+            q, k, v = src[base, own, lanes], src[base + 1, keys, lanes], src[base + 2, keys, lanes]
             do = DO[own, lanes]
             low_q = lax.broadcasted_iota(jnp.int32, q.shape, 1) < 64
             high_q = lax.broadcasted_iota(jnp.int32, q.shape, 1) >= 64
@@ -764,19 +765,17 @@
 
         loop(HEADS // 2, pair)
 
-    def out_project(o_index, which):
-        for s in (0, 1):
-            own = span[s]
-
-            def tile(i):
-                RES[own, cols(i, 256)] = HID[own, cols(i, 256)] + dot(
-                    S[o_index, own], wtile(s, UB[which], i)
-                )
-
-            loop(NT, tile)
+    def out_project(o_index, which, s):
+        own = span[s]
+
+        def tile(i):
+            RES[own, cols(i, 256)] = HID[own, cols(i, 256)] + dot(
+                S[o_index, own], wtile(s, UB[which], i)
+            )
+
+        loop(NT, tile)
 
     RB = 16
-    NB0 = T0 // RB
     mean = lambda v: jnp.sum(v, axis=-1, keepdims=True) * (1.0 / D)
 
     def normalize(i, r):
@@ -785,13 +784,12 @@
         rstd = lax.rsqrt(mean(centre * centre) + 1e-05)
         return centre * rstd, rstd
 
-    def row_of(i, s):
-        return vecs[pl.ds(s * 3 + i, 1), :]
-
-    def norm_forward(i, h_index):
+    def rows_of(s, b):
+        return pl.ds(pl.multiple_of((0, T0)[s] + b * RB, RB), RB)
+
+    def norm_forward(i, h_index, s):
         def block(b):
-            s = b // NB0
-            r = cols(b, RB)
+            r = rows_of(s, b)
             xh, rstd = normalize(i, r)
             XH[i, r] = xh
             RSTD[i, r] = rstd
@@ -799,7 +797,7 @@
             HID[r] = hidden
             S[h_index, r] = hidden.astype(BF)
 
-        loop(T // RB, block)
+        loop(size[s] // RB, block)
 
     def add_row(row, value):
         VG[pl.ds(row, 1), :] += jnp.sum(value, axis=0, keepdims=True)
@@ -810,20 +808,18 @@
         dx = dh * vecs[pl.ds(s * 3 + i, 1), :]
         return rstd * (dx - mean(dx) - xh * mean(dx * xh))
 
-    def norm_backward(i, g_index):
+    def norm_backward(i, g_index, s):
         def block(b):
-            s = b // NB0
-            r = cols(b, RB)
+            r = rows_of(s, b)
             dr = norm_pull(i, s, r, DR[r], XH[i, r], RSTD[i, r])
             DR[r] = dr
             S[g_index, r] = dr.astype(BF)
 
-        loop(T // RB, block)
-
-    def tail():
+        loop(size[s] // RB, block)
+
+    def tail(s):
         def block(b):
-            s = b // NB0
-            r = cols(b, RB)
+            r = rows_of(s, b)
             xh, rstd = normalize(2, r)
             gain = vecs[pl.ds(s * 3 + 2, 1), :]
             h3 = xh * gain + vecs[pl.ds(6 + s * 3 + 2, 1), :]
@@ -831,9 +827,7 @@
             logit = jnp.sum(h3 * gate, axis=-1, keepdims=True)
             sig = 1.0 / (1.0 + jnp.exp(-logit))
             index = lax.broadcasted_iota(jnp.int32, (RB, 1), 0) + b * RB
-            text = index < T0
-            mask = (text & live(index, 0)) | ((index >= T0) & live(index - T0, 1))
-            mask = jnp.where(mask, 1.0, 0.0)
+            mask = jnp.where(live(index, s), 1.0, 0.0)
             weight = sig * mask
             HID[r] = h3 * weight
             dout = DR[r]
@@ -843,101 +837,98 @@
             DR[r] = dr
             S[DF, r] = dr.astype(BF)
 
-        loop(T // RB, block)
+        loop(size[s] // RB, block)
         o_ta, o_va, o_tb, o_vb = outs
-        o_ta[0] = HID[0:la].astype(BF)
-        o_tb[0] = HID[la : la + g.lb].astype(BF)
-        o_va[0] = HID[T0 : T0 + lva].astype(BF)
-        o_vb[0] = HID[T0 + lva : T0 + lva + g.lvb].astype(BF)
-
-    def ffn_up(q):
-        for s in (0, 1):
-            own = span[s]
-
-            def tile(i):
-                j = q * NT + i
-                u = dot(S[H2, own], wtile(s, 8 + q, i))
-                cdf = 0.5 + 0.5 * erf_of(u * 0.7071067811865476)
-                A[own, cols(j, 256)] = (u * cdf).astype(BF)
-                GP[own, cols(j, 256)] = cdf + u * (
-                    jnp.exp(u * u * -0.5) * 0.3989422804014327
-                )
-
-            loop(NT, tile)
-
-    def ffn_down():
-        for s in (0, 1):
-            own = span[s]
-
-            def tile(i):
-                total = HID[own, cols(i, 256)]
-                for q in range(4):
-                    total = total + dot(A[own, D * q : D * q + D], wtile(s, 12 + q, i))
-                RES[own, cols(i, 256)] = total
-
-            loop(NT, tile)
-
-    def ffn_down_back():
-        for s in (0, 1):
-            own = span[s]
-
-            def tile(j):
-                da = dot_rt(S[DF, own], wrows(s, 12 + j // NT, j % NT))
-                DU[own, cols(j, 256)] = (GP[own, cols(j, 256)] * da).astype(BF)
-
-            loop(4 * NT, tile)
-
-    def ffn_up_back():
-        for s in (0, 1):
-            own = span[s]
-
-            def tile(i):
-                total = DR[own, cols(i, 256)]
-                for q in range(4):
-                    total = total + dot_rt(DU[own, D * q : D * q + D], wrows(s, 8 + q, i))
-                DR[own, cols(i, 256)] = total
-
-            loop(NT, tile)
-
-    def out_back(g_index, which):
-        for s in (0, 1):
-            own = span[s]
-
-            def tile(i):
-                DO[own, cols(i, 256)] = dot_rt(
-                    S[g_index, own], wrows(s, UB[which], i)
-                ).astype(BF)
-
-            loop(NT, tile)
-
-    def self_back():
-        for s in (0, 1):
-            own = span[s]
-
-            def tile(i):
-                total = DR[own, cols(i, 256)]
-                for m, gi in enumerate((DQS, DKS, DVS)):
-                    total = total + dot_rt(S[gi, own], wrows(s, 4 + m, i))
-                DR[own, cols(i, 256)] = total
-
-            loop(NT, tile)
-
-    def cross_back():
-        for s in (0, 1):
-            own = span[s]
-
-            def tile(i):
-                total = DR[own, cols(i, 256)] + dot_rt(S[DQC, own], wrows(s, 0, i))
-                total = total + dot_rt(S[DKC, own], wrows(1 - s, 1, i))
-                total = total + dot_rt(S[DVC, own], wrows(1 - s, 2, i))
-                DR[own, cols(i, 256)] = total
-
-            loop(NT, tile)
+        if s == 0:
+            o_ta[0] = HID[0:la].astype(BF)
+            o_tb[0] = HID[la : la + g.lb].astype(BF)
+        else:
+            o_va[0] = HID[T0 : T0 + lva].astype(BF)
+            o_vb[0] = HID[T0 + lva : T0 + lva + g.lvb].astype(BF)
+
+    def ffn_up(q, s):
+        own = span[s]
+
+        def tile(i):
+            j = q * NT + i
+            u = dot(S[H2, own], wtile(s, 8 + q, i))
+            cdf = 0.5 + 0.5 * erf_of(u * 0.7071067811865476)
+            A[own, cols(j, 256)] = (u * cdf).astype(BF)
+            GP[own, cols(j, 256)] = cdf + u * (
+                jnp.exp(u * u * -0.5) * 0.3989422804014327
+            )
+
+        loop(NT, tile)
+
+    def ffn_down(s):
+        own = span[s]
+
+        def tile(i):
+            total = HID[own, cols(i, 256)]
+            for q in range(4):
+                total = total + dot(A[own, D * q : D * q + D], wtile(s, 12 + q, i))
+            RES[own, cols(i, 256)] = total
+
+        loop(NT, tile)
+
+    def ffn_down_back(s):
+        own = span[s]
+
+        def tile(j):
+            da = dot_rt(S[DF, own], wrows(s, 12 + j // NT, j % NT))
+            DU[own, cols(j, 256)] = (GP[own, cols(j, 256)] * da).astype(BF)
+
+        loop(4 * NT, tile)
+
+    def ffn_up_back(s):
+        own = span[s]
+
+        def tile(i):
+            total = DR[own, cols(i, 256)]
+            for q in range(4):
+                total = total + dot_rt(DU[own, D * q : D * q + D], wrows(s, 8 + q, i))
+            DR[own, cols(i, 256)] = total
+
+        loop(NT, tile)
+
+    def out_back(g_index, which, s):
+        own = span[s]
+
+        def tile(i):
+            DO[own, cols(i, 256)] = dot_rt(
+                S[g_index, own], wrows(s, UB[which], i)
+            ).astype(BF)
+
+        loop(NT, tile)
+
+    def self_back(s):
+        own = span[s]
+
+        def tile(i):
+            total = DR[own, cols(i, 256)]
+            for m, gi in enumerate((DQS, DKS, DVS)):
+                total = total + dot_rt(S[gi, own], wrows(s, 4 + m, i))
+            DR[own, cols(i, 256)] = total
+
+        loop(NT, tile)
+
+    def cross_back(s):
+        own = span[s]
+
+        def tile(i):
+            total = DR[own, cols(i, 256)] + dot_rt(S[DQC, own], wrows(s, 0, i))
+            total = total + dot_rt(S[DKC, own], wrows(1 - s, 1, i))
+            total = total + dot_rt(S[DVC, own], wrows(1 - s, 2, i))
+            DR[own, cols(i, 256)] = total
+
+        loop(NT, tile)
         g_ta, g_va, g_tb, g_vb = grads
-        g_ta[0] = DR[0:la].astype(BF)
-        g_tb[0] = DR[la : la + g.lb].astype(BF)
-        g_va[0] = DR[T0 : T0 + lva].astype(BF)
-        g_vb[0] = DR[T0 + lva : T0 + lva + g.lvb].astype(BF)
+        if s == 0:
+            g_ta[0] = DR[0:la].astype(BF)
+            g_tb[0] = DR[la : la + g.lb].astype(BF)
+        else:
+            g_va[0] = DR[T0 : T0 + lva].astype(BF)
+            g_vb[0] = DR[T0 + lva : T0 + lva + g.lvb].astype(BF)
 
     sends = []
 
@@ -971,167 +962,211 @@
             def _():
                 pltpu.make_async_copy(ref, ref, s_own.at[slot]).wait()
 
-    A_OF = (X, X, X, H1, H1, H1, OC, OS)
-    G_OF = (DQC, DKC, DVC, DQS, DKS, DVS, DC, DS)
+    A_OF = (X, X, X, OC, H1, H1, H1, OS)
+    G_OF = (DQC, DKC, DVC, DC, DQS, DKS, DVS, DS)
     HB = D // 2
 
-    def send_left(r):
-        plane_send(r, S.at[A_OF[r]], ra.at[me], 0)
-
-    def send_right(r):
-        plane_send(r, S.at[G_OF[r]], rg.at[me], 1)
-
-    def send_ffn_left(r):
+    def rows_for(r, s):
+        t = 1 - s if r in (1, 2) else s
+        return pl.ds((0, T0)[t], size[t])
+
+    def send_left(r, s):
+        rows = rows_for(r, s)
+        plane_send(r, S.at[A_OF[r], rows], ra.at[me, rows], 7 * s)
+
+    def send_right(r, s):
+        rows = rows_for(r, s)
+        plane_send(r, S.at[G_OF[r], rows], rg.at[me, rows], 7 * s + 1)
+
+    def own_rows(s):
+        return pl.ds((0, T0)[s], size[s])
+
+    def send_ffn_left(r, q, s):
+        rows = own_rows(s)
         if r < 4:
-            plane_send(r, S.at[H2], rfa.at[me, :, pl.ds(0, D)], 3)
+            plane_send(r, S.at[H2, rows], rfa.at[me, rows, pl.ds(0, D)], 7 * s + 3)
         else:
-            yy = (r - 4) // 2
+            plane_send(
+                r, A.at[rows, pl.ds(D * q + HB * (r % 2), HB)],
+                rfa.at[me, rows, pl.ds(HB * q, HB)], 7 * s + 3 + q,
+            )
+
+    def send_ffn_right(r, s):
+        rows = own_rows(s)
+        if r < 4:
+            plane_send(r, DU.at[rows, pl.ds(D * r, D)], rfg.at[me, rows], 7 * s + 2)
+        else:
+            hh = (r // 2) % 2
+            plane_send(
+                r, S.at[DF, rows, pl.ds(HB * hh, HB)], rfg.at[me, rows, pl.ds(0, HB)], 7 * s + 2
+            )
+
+    flip = (((me + 1) // 2) % 2) * (1 - me // 4)
+
+    def stage(s, rows, n, first, blocks):
+        made = []
+        for src, unit, col in blocks:
+            for p in range(8):
+                made.append(
+                    pltpu.make_async_copy(
+                        src.at[p, rows, pl.ds(col, D)],
+                        W.at[s, unit + p // 4, pl.ds(n * (p % 4), n)],
+                        s_st.at[first + len(made)],
+                    )
+                )
+        for cp in made:
+            cp.start()
+        for cp in made:
+            cp.wait()
+
+    def stacked(s, unit, n, lanes):
+        return jnp.concatenate(
+            [W[s, unit + p // 4, n * (p % 4) : n * (p % 4) + n, lanes] for p in range(8)], axis=0
+        )
+
+    def weight_grad(s, n, dst):
+        def tile(i):
+            W[s, dst, cols(i, 256), :] = dot_lt(
+                stacked(s, 8, n, cols(i, 256)), stacked(s, 12, n, slice(0, D))
+            ).astype(BF)
+
+        loop(NT, tile)
+
+    def weight_grad_down(s, n, dst):
+        def tile(q):
+            out = dot_lt(
+                stacked(s, 8 + 2 * (q // 2), n, cols(q % 2, HB)), stacked(s, 12, n, slice(0, HB))
+            ).astype(BF)
+            W[s, dst, pl.ds(pl.multiple_of(q * ZR, ZR), ZR), 0:HB] = out[0:ZR]
+            W[s, dst, pl.ds(pl.multiple_of(q * ZR, ZR), ZR), HB:D] = out[ZR : 2 * ZR]
+
+        loop(4, tile)
+
+    def z_send(n, s, d):
+        zz = (z + d) % NZ
+        src = W.at[s, 14 + n, pl.ds(pl.multiple_of(zz * ZR, ZR), ZR)]
+        return remote(
+            src, RZ.at[n, s, d - 1], s_zr.at[n, s, d - 1], r_zr.at[n, s, d - 1],
+            device(x, zz, y, c),
+        )
+
+    def z_collect(n, s):
+        for d in range(1, NZ):
+            z_send(n, s, d).wait_recv()
+
+        def block(i):
+            total = W[s, 14 + n, pl.ds(pl.multiple_of(z * ZR + i * 16, 16), 16)].astype(F32)
+            for d in range(NZ - 1):
+                total = total + RZ[n, s, d, cols(i, 16)].astype(F32)
+            FB[n, s, cols(i, 16)] = total.astype(BF)
+
+        loop(ZR // 16, block)
+
+    def ffn_share(s):
+        rows, n = own_rows(s), size[s]
+
+        @pl.when(me < 4)
+        def _():
+            plane_wait(7 * s + 2, lambda p: rfg.at[p, rows])
+            plane_wait(7 * s + 3, lambda p: rfa.at[p, rows, pl.ds(0, D)])
+
+        @pl.when(me >= 4)
+        def _():
+            plane_wait(7 * s + 2, lambda p: rfg.at[p, rows, pl.ds(0, HB)])
             for q in range(4):
-                plane_send(
-                    r, A.at[:, pl.ds(D * q + HB * yy, HB)], rfa.at[me, :, pl.ds(HB * q, HB)],
-                    3 + q,
-                )
-
-    def send_ffn_right(r):
-        if r < 4:
-            plane_send(r, DU.at[:, pl.ds(D * r, D)], rfg.at[me], 2)
-        else:
-            hh = (r - 4) % 2
-            plane_send(r, S.at[DF, :, pl.ds(HB * hh, HB)], rfg.at[me, :, pl.ds(0, HB)], 2)
-
-    st = [0]
-
-    def stage(src, dst_unit, col, width, dcol):
-        copies = []
-        for half in range(2):
-            for p in range(4):
-                cp = pltpu.make_async_copy(
-                    src.at[4 * half + p, :, pl.ds(col, width)],
-                    W.at[half, dst_unit, pl.ds(T * p, T), pl.ds(dcol, width)],
-                    s_st.at[st[0]],
-                )
-                st[0] += 1
-                cp.start()
-                copies.append(cp)
-        return copies
-
-    def stacked(unit, rs, lanes):
-        first, count = (0, T0) if rs == 0 else (T0, T1)
-        return jnp.concatenate(
-            [
-                W[half, unit, T * p + first : T * p + first + count, lanes]
-                for half in range(2)
-                for p in range(4)
-            ],
-            axis=0,
-        )
-
-    def weight_grad(left, right, dst):
-        for rs in range(2):
-
-            def tile(i):
-                W[rs, dst, cols(i, 256), :] = dot_lt(
-                    stacked(left, rs, cols(i, 256)), stacked(right, rs, slice(0, D))
-                ).astype(BF)
-
-            loop(NT, tile)
-
-    def weight_grad_down(right, dst):
-        for rs in range(2):
-
-            def tile(q):
-                left_unit = 10 + q // 2
-                out = dot_lt(
-                    stacked(left_unit, rs, cols(q % 2, HB)), stacked(right, rs, slice(0, HB))
-                ).astype(BF)
-                W[rs, dst, pl.ds(pl.multiple_of(q * ZR, ZR), ZR), 0:HB] = out[0:ZR]
-                W[rs, dst, pl.ds(pl.multiple_of(q * ZR, ZR), ZR), HB:D] = out[ZR : 2 * ZR]
-
-            loop(4, tile)
-
-    def z_send(n, unit, d):
-        zz = (z + d) % NZ
-        src = W.at[:, unit, pl.ds(pl.multiple_of(zz * ZR, ZR), ZR)]
-        return remote(src, RZ.at[n, d - 1], s_zr.at[n, d - 1], r_zr.at[n, d - 1], device(x, zz, y, c))
-
-    def z_collect(n, unit):
+                plane_wait(7 * s + 3 + q, lambda p: rfa.at[p, rows, pl.ds(HB * q, HB)])
+
+        stage(s, rows, n, 0, ((rfg, 12, 0), (rfa, 8, 0), (rfa, 10, D)))
+
+        @pl.when(me < 4)
+        def _():
+            weight_grad(s, n, 15)
+
+        @pl.when(me >= 4)
+        def _():
+            weight_grad_down(s, n, 15)
+
         for d in range(1, NZ):
-            z_send(n, unit, d).wait_recv()
-        for rs in range(2):
-
-            def block(i):
-                total = W[rs, unit, pl.ds(pl.multiple_of(z * ZR + i * 16, 16), 16)].astype(F32)
-                for d in range(NZ - 1):
-                    total = total + RZ[n, d, rs, cols(i, 16)].astype(F32)
-                FB[n, rs, cols(i, 16)] = total.astype(BF)
-
-            loop(ZR // 16, block)
-
-    flip = (((me + 1) // 2) % 2) * (1 - (me // 3 + 1) // 2)
-
-    def attn_blocks(r):
-        yy, cc = (r // 2) % 2, r % 2
-        for rs in range(2):
-            src = FB.at[0, rs, pl.ds(R * (2 * yy + cc), R)]
-            s = rs + flip - 2 * rs * flip
-            yield rs, src, ga.at[s, me]
-
-    def up_blocks(r):
-        yy, cc = (r // 2) % 2, r % 2
-        for rs in range(2):
-            src = FB.at[1, rs, pl.ds(R * (2 * yy + cc), R)]
-            yield 2 + rs, src, gu.at[rs, :, pl.ds(pl.multiple_of(D * (me % 4), 128), D)]
-
-    def down_blocks(r):
-        cc = r % 2
-        for rs in range(2):
-            src = FB.at[1, rs, :, pl.ds(HB * cc, HB)]
-            yield 2 + rs, src, gd.at[rs, :, pl.ds(pl.multiple_of(HB * (me % 2), 128), HB)]
-
-    def spread(r, blocks, cond, act):
-        for n, src, dst in blocks(r):
-
-            @pl.when(cond & (me != r))
-            def _():
-                cp = remote(src, dst, s_rd.at[n, r], r_rd.at[n, me], role_device(r))
-                cp.start() if act == "start" else cp.wait_send()
-
-            @pl.when(cond & (me == r))
-            def _():
-                cp = pltpu.make_async_copy(src, dst, s_own.at[8 + n])
-                cp.start() if act == "start" else cp.wait()
-
-    def spread_all(n, act):
+            z_send(1, s, d).start()
+
+    def attention_share(s):
+        def branch(r):
+            rows, n = rows_for(r, s), size[1 - s if r in (1, 2) else s]
+            plane_wait(7 * s, lambda p: ra.at[p, rows])
+            plane_wait(7 * s + 1, lambda p: rg.at[p, rows])
+            stage(s, rows, n, 24, ((ra, 8, 0), (rg, 12, 0)))
+            weight_grad(s, n, 14)
+
+        @pl.when(flip == 0)
+        def _():
+            branch(0)
+
+        @pl.when(flip == 1)
+        def _():
+            branch(1)
+
+        for d in range(1, NZ):
+            z_send(0, s, d).start()
+
+    slot_of = me + 3 * (me // 3) * (1 - me // 4) - (me // 4) * (1 - me // 7)
+
+    def attn_block(r, s):
+        return FB.at[0, s, pl.ds(R * (2 * (r % 2) + r // 4), R)], ga.at[s, slot_of]
+
+    def up_block(r, s):
+        return (
+            FB.at[1, s, pl.ds(R * (2 * (r % 2) + r // 4), R)],
+            gu.at[s, :, pl.ds(pl.multiple_of(D * (me % 4), 128), D)],
+        )
+
+    def down_block(r, s):
+        return (
+            FB.at[1, s, :, pl.ds(HB * (r // 4), HB)],
+            gd.at[s, :, pl.ds(pl.multiple_of(HB * ((me // 2) % 2), 128), HB)],
+        )
+
+    def spread(r, n, s, block, cond, act):
+        src, dst = block(r, s)
+
+        @pl.when(cond & (me != r))
+        def _():
+            cp = remote(src, dst, s_rd.at[2 * n + s, r], r_rd.at[2 * n + s, me], role_device(r))
+            cp.start() if act == "start" else cp.wait_send()
+
+        @pl.when(cond & (me == r))
+        def _():
+            cp = pltpu.make_async_copy(src, dst, s_own.at[14 + 2 * n + s])
+            cp.start() if act == "start" else cp.wait()
+
+    def spread_all(n, s, act):
         for r in range(8):
             if n == 0:
-                spread(r, attn_blocks, me >= 0, act)
+                spread(r, n, s, attn_block, me >= 0, act)
             else:
-                spread(r, up_blocks, me < 4, act)
-                spread(r, down_blocks, (me // 2 == 2 + (r // 2) % 2), act)
+                spread(r, n, s, up_block, me < 4, act)
+                spread(r, n, s, down_block, (me >= 4) & (me % 2 == r % 2), act)
 
     def spread_wait():
+        def arrived(ref, n, s, p):
+            remote(
+                ref, ref, s_rd.at[2 * n + s, p], r_rd.at[2 * n + s, p], role_device(p)
+            ).wait_recv()
+
         for p in range(8):
 
             @pl.when(me != p)
             def _():
-                for rs in range(2):
-                    ref = ga.at[rs, p]
-                    remote(ref, ref, s_rd.at[rs, p], r_rd.at[rs, p], role_device(p)).wait_recv()
+                for s in range(2):
+                    arrived(ga.at[s, p], 0, s, p)
                     if p < 4:
-                        ref = gu.at[rs, :, pl.ds(D * p, D)]
-                        remote(
-                            ref, ref, s_rd.at[2 + rs, p], r_rd.at[2 + rs, p], role_device(p)
-                        ).wait_recv()
+                        arrived(gu.at[s, :, pl.ds(D * p, D)], 1, s, p)
 
             if p >= 4:
 
-                @pl.when((me != p) & (y == (p - 4) // 2))
+                @pl.when((me != p) & (y == p % 2))
                 def _():
-                    for rs in range(2):
-                        ref = gd.at[rs, :, pl.ds(HB * (p % 2), HB)]
-                        remote(
-                            ref, ref, s_rd.at[2 + rs, p], r_rd.at[2 + rs, p], role_device(p)
-                        ).wait_recv()
+                    for s in range(2):
+                        arrived(gd.at[s, :, pl.ds(HB * (p % 2), HB)], 1, s, p)
 
     VG[...] = jnp.zeros_like(VG)
     for step in range(1, g.fsdp):
@@ -1145,26 +1180,15 @@
         total = total + dot(VEC[ff], pick)
     vecs[...] = total
 
-    gather_steps(0, 7)
-    cross_project()
-    gather_steps(7, 8)
-    attend(CQ, 0, 1, p_refs[0], OC)
-    attend(CQ, 1, 0, p_refs[1], OC)
-    gather_steps(8, 9)
-    out_project(OC, 0)
-    norm_forward(0, H1)
-    gather_steps(9, 11)
-    self_project()
-    gather_steps(11, 12)
-    attend(SQ, 0, 0, p_refs[2], OS)
-    attend(SQ, 1, 1, p_refs[3], OS)
-    gather_steps(12, 13)
-    out_project(OS, 1)
-    norm_forward(1, H2)
-    gather_steps(13, 15)
-    for q in range(4):
-        gather_steps(15 + q, 16 + q)
-        ffn_up(q)
+    reached = [0]
+
+    def gather_to(t):
+        if t > reached[0]:
+            gather_steps(reached[0], t)
+            reached[0] = t
+
+    def gather_more(n):
+        gather_to(min(reached[0] + n, NK + 3))
 
     def gather_sent(k):
         for d in range(1, NZ):
@@ -1176,34 +1200,70 @@
                 if d or e:
                     x_copy(k, d, e).wait_send()
 
-    loop(16, gather_sent)
-    for r in range(8):
-        send_ffn_left(r)
-    for r in range(8):
-        send_left(r)
-    ffn_down()
-    tail()
-    for r in range(4, 8):
-        send_ffn_right(r)
-    ffn_down_back()
-    for r in range(4):
-        send_ffn_right(r)
-    ffn_up_back()
-    norm_backward(1, DS)
-    send_right(7)
-    out_back(DS, 1)
-    attend_back(SQ, 0, 0, p_refs[2], DQS, DKS, DVS)
-    attend_back(SQ, 1, 1, p_refs[3], DQS, DKS, DVS)
-    for r in (3, 4, 5):
-        send_right(r)
-    self_back()
-    norm_backward(0, DC)
-    send_right(6)
-    out_back(DC, 0)
-    attend_back(CQ, 0, 1, p_refs[0], DQC, DKC, DVC)
-    attend_back(CQ, 1, 0, p_refs[1], DQC, DKC, DVC)
-    for r in (0, 1, 2):
-        send_right(r)
+    for s in range(2):
+        base = 16 * s + 4
+        gather_to(base + 2)
+        cross_project(s)
+        gather_to(base + 3)
+        attend(CQ, 0, s, 1 - s, p_refs[s], OC)
+        if s == 1:
+            z_collect(1, 0)
+            spread_all(1, 0, "start")
+        gather_to(base + 4)
+        out_project(OC, 0, s)
+        norm_forward(0, H1, s)
+        gather_to(base + 6)
+        self_project(s)
+        gather_to(base + 7)
+        attend(SQ, 0, s, s, p_refs[2 + s], OS)
+        if s == 1:
+            z_collect(0, 0)
+            spread_all(0, 0, "start")
+        gather_to(base + 8)
+        out_project(OS, 1, s)
+        norm_forward(1, H2, s)
+        for r in range(4):
+            send_ffn_left(r, 0, s)
+        for q in range(4):
+            gather_to(base + 8 + q)
+            ffn_up(q, s)
+            for r in range(4, 8):
+                send_ffn_left(r, q, s)
+        gather_to(base + 15)
+        ffn_down(s)
+        gather_more(1)
+        tail(s)
+        for r in range(4, 8):
+            send_ffn_right(r, s)
+        gather_more(1)
+        ffn_down_back(s)
+        for r in range(4):
+            send_ffn_right(r, s)
+        for r in range(8):
+            send_left(r, s)
+        gather_more(1)
+        ffn_up_back(s)
+        norm_backward(1, DS, s)
+        send_right(7, s)
+        gather_more(1)
+        out_back(DS, 1, s)
+        attend_back(SQ, 0, s, s, p_refs[2 + s], DQS, DKS, DVS)
+        for r in (4, 5, 6):
+            send_right(r, s)
+        gather_more(1)
+        lax.fori_loop(16 * s, 16 * s + 16, lambda k, carry: (gather_sent(k), carry)[1], 0)
+        ffn_share(s)
+        gather_more(1)
+        self_back(s)
+        norm_backward(0, DC, s)
+        send_right(3, s)
+        gather_more(1)
+        out_back(DC, 0, s)
+        attend_back(CQ, 0, s, 1 - s, p_refs[s], DQC, DKC, DVC)
+        for r in (0, 1, 2):
+            send_right(r, s)
+        gather_more(1)
+        attention_share(s)
 
     def vg_copy(r):
         return remote(VG, VR.at[me], s_vg.at[r], r_vg.at[me], role_device(r))
@@ -1215,42 +1275,8 @@
             vg_copy(r).start()
 
     VR[me] = VG[...]
-    cross_back()
-
-    @pl.when(me < 4)
-    def _():
-        plane_wait(2, lambda p: rfg.at[p])
-        plane_wait(3, lambda p: rfa.at[p, :, pl.ds(0, D)])
-
-    @pl.when(me >= 4)
-    def _():
-        plane_wait(2, lambda p: rfg.at[p, :, pl.ds(0, HB)])
-        for q in range(4):
-            plane_wait(3 + q, lambda p: rfa.at[p, :, pl.ds(HB * q, HB)])
-
-    copies = stage(rfg, 12, 0, D, 0) + stage(rfa, 10, 0, D, 0) + stage(rfa, 11, D, D, 0)
-    for cp in copies:
-        cp.wait()
-
-    @pl.when(me < 4)
-    def _():
-        weight_grad(10, 12, 15)
-
-    @pl.when(me >= 4)
-    def _():
-        weight_grad_down(12, 15)
-
-    for d in range(1, NZ):
-        z_send(1, 15, d).start()
-
-    plane_wait(0, lambda p: ra.at[p])
-    plane_wait(1, lambda p: rg.at[p])
-    copies = stage(ra, 8, 0, D, 0) + stage(rg, 9, 0, D, 0)
-    for cp in copies:
-        cp.wait()
-    weight_grad(8, 9, 14)
-    for d in range(1, NZ):
-        z_send(0, 14, d).start()
+    cross_back(0)
+    cross_back(1)
 
     for p in range(8):
 
@@ -1271,8 +1297,8 @@
 
     for d in range(1, NZ):
         vz_copy(d).start()
-    z_collect(1, 15)
-    spread_all(1, "start")
+    z_collect(1, 1)
+    spread_all(1, 1, "start")
     for d in range(1, NZ):
         ref = VZ.at[(z + NZ - d) % NZ]
         remote(ref, ref, s_vz.at[d - 1], r_vz.at[d - 1], device(x, z, y, c)).wait_recv()
@@ -1280,8 +1306,8 @@
     for zz in range(1, NZ):
         total = total + VZ[zz]
     vec_out[...] = total
-    z_collect(0, 14)
-    spread_all(0, "start")
+    z_collect(0, 1)
+    spread_all(0, 1, "start")
 
     for step in range(1, g.fsdp):
         vec_copy(step).wait_send()
@@ -1294,11 +1320,13 @@
 
     for d in range(1, NZ):
         vz_copy(d).wait_send()
-        z_send(0, 14, d).wait_send()
-        z_send(1, 15, d).wait_send()
+        for n in range(2):
+            for s in range(2):
+                z_send(n, s, d).wait_send()
     spread_wait()
-    spread_all(1, "wait")
-    spread_all(0, "wait")
+    for n in range(2):
+        for s in range(2):
+            spread_all(n, s, "wait")
 
 
 def kernel_path(g, *args):
@@ -1344,28 +1372,28 @@
         vmem(HEADS, T1, T0, F32),
         vmem(HEADS, T0, T0, F32),
         vmem(HEADS, T1, T1, F32),
-        vmem(2, NZ - 1, 2, D // NZ, D, BF),
+        vmem(2, 2, NZ - 1, D // NZ, D, BF),
         vmem(2, 2, D // NZ, D, BF),
         vmem(16, D, F32),
         vmem(8, 16, D, F32),
         vmem(NZ, 16, D, F32),
-        dma(17),
+        dma(33),
         dma(g.fsdp - 1),
         dma(g.fsdp - 1),
-        dma(16, NZ - 1),
-        dma(16, NZ - 1),
-        dma(16, NZ),
-        dma(16, NZ),
-        dma(16, 2 * NZ),
-        dma(16, 2 * NZ),
-        dma(16, 2 * NZ),
-        dma(16, 2 * NZ),
-        dma(7, 8),
-        dma(7, 8),
-        dma(12),
+        dma(32, NZ - 1),
+        dma(32, NZ - 1),
+        dma(32, NZ),
+        dma(32, NZ),
+        dma(32, 2 * NZ),
+        dma(32, 2 * NZ),
+        dma(32, 2 * NZ),
+        dma(32, 2 * NZ),
+        dma(14, 8),
+        dma(14, 8),
+        dma(18),
         dma(40),
-        dma(2, NZ - 1),
-        dma(2, NZ - 1),
+        dma(2, 2, NZ - 1),
+        dma(2, 2, NZ - 1),
         dma(4, 8),
         dma(4, 8),
         dma(8),

time: 422 us -> 396 us (0.938); the launches traced: 415 us -> 396 us
  Pallas kernels: 395 us -> 376 us
    pallas_call x1, Pallas kernels: 395 us -> 376 us  [kernel_path(): pl.pallas_call(partial(layer_kernel, g), out_shape=out_shape, in_specs=[i...]
where the time goes in v3:
time: 396 us
  Pallas kernels  376 us (95%)
  local copies, waits for them, and re-layouts  13.3 us (3%)
    pallas_call x1, Pallas kernels, kernel_path(): pl.pallas_call(partial(layer_kernel, g), out_shape=out_shape, in_specs=[i...  376 us

profile of v3, /device:TPU:31, one launch (start us, length us, event | category | flops | bytes accessed | tf_op | source)
XLA Modules:
  0.0 395.7 jit_solution(17807483508212751205)
XLA Ops:
  0.6 0.7 copy.38
  1.3 0.7 copy.39
  2.1 1.3 fusion.8.refs_16_
  5.9 375.7 %layer.1 = (bf16[1,48,768]{2,1,0:T(8,128)(2,1)}, bf16[1,20,768]{2,1,0:T(8,128)(2,1)}, bf16[1,56,768]{2,1,0:T(8,128)(2,1)}, bf16[1,28,768]{2,1,0:T(8,128)(2,1)}, ...) custom-call(s32[1]{0:T(128)S(6)} %copy.50.refs_0_, ...), custom_call_target="tpu_custom_call" | custom-call | tf_op jit(solution)/shard_map/layer/pallas_call | solution.py:1404
  381.6 0.0 copy-start
  381.6 0.9 fusion.9
  382.5 0.6 copy.40
  383.1 0.6 copy.41
  383.6 1.3 dynamic-slice.2
  385.0 0.0 copy-start.2
  385.0 2.6 slice.20
  387.6 0.0 copy-done
  387.6 0.0 copy-start.1
  387.6 0.9 slice.21
  388.4 0.0 copy-start.6
  388.4 0.0 copy-start.10
  388.4 0.0 copy-start.4
  388.4 0.0 copy-done.2
  388.4 0.0 copy-start.8
  388.4 0.0 copy-start.5
  388.5 0.0 copy-start.9
  388.5 0.0 copy-start.3
  388.5 0.0 copy-start.7
  388.5 1.1 convert_element_type.12
  389.6 0.0 copy-done.1
  389.6 1.1 convert_element_type.13
  390.7 0.0 copy-done.6
  390.7 0.6 copy.54
  391.3 0.0 copy-done.10
  391.3 0.6 copy.55
  392.0 0.0 copy-done.4
  392.0 0.6 copy.56
  392.6 0.0 copy-done.8
  392.6 0.6 copy.57
  393.2 0.0 copy-done.5
  393.2 0.6 copy.58
  393.8 0.0 copy-done.9
  393.9 0.6 copy.59
  394.5 0.0 copy-done.3
  394.5 0.6 copy.60
  395.1 0.0 copy-done.7
  395.1 0.6 copy.61
  (4 shorter events, 0.1 us)
Async XLA Ops:
  381.6 6.0 %copy-start = (bf16[2,8,48,768]{3,2,1,0:T(8,128)(2,1)S(1)}, bf16[2,8,48,768]{3,2,1,0:T(8,128)(2,1)}, u32[]{:S(2)}) copy-start(bf16[2,8,48,768]{3,2,1,0:T(8,128)(2,1)} %get-tuple-element.35) | copy-start | bytes 3538948
  385.0 3.5 copy-start.2
  387.6 2.0 copy-start.1
  388.4 2.3 copy-start.6
  388.4 2.9 copy-start.10
  388.4 3.5 copy-start.4
  388.4 4.2 %copy-start.8 = (bf16[1,28,768]{2,1,0:T(8,128)(2,1)S(1)}, bf16[1,28,768]{2,1,0:T(8,128)(2,1)}, u32[]{:S(2)}) copy-start(bf16[1,28,768]{2,1,0:T(8,128)(2,1)} %get-tuple-element.89) | copy-start | bytes 129028
  388.4 4.8 %copy-start.5 = (bf16[1,48,768]{2,1,0:T(8,128)(2,1)S(1)}, bf16[1,48,768]{2,1,0:T(8,128)(2,1)}, u32[]{:S(2)}) copy-start(bf16[1,48,768]{2,1,0:T(8,128)(2,1)} %get-tuple-element.90) | copy-start | bytes 221188
  388.5 5.4 %copy-start.9 = (bf16[1,20,768]{2,1,0:T(8,128)(2,1)S(1)}, bf16[1,20,768]{2,1,0:T(8,128)(2,1)}, u32[]{:S(2)}) copy-start(bf16[1,20,768]{2,1,0:T(8,128)(2,1)} %get-tuple-element.91) | copy-start | bytes 92164
  388.5 6.0 %copy-start.3 = (bf16[1,56,768]{2,1,0:T(8,128)(2,1)S(1)}, bf16[1,56,768]{2,1,0:T(8,128)(2,1)}, u32[]{:S(2)}) copy-start(bf16[1,56,768]{2,1,0:T(8,128)(2,1)} %get-tuple-element.92) | copy-start | bytes 258052
  388.5 6.6 %copy-start.7 = (bf16[1,28,768]{2,1,0:T(8,128)(2,1)S(1)}, bf16[1,28,768]{2,1,0:T(8,128)(2,1)}, u32[]{:S(2)}) copy-start(bf16[1,28,768]{2,1,0:T(8,128)(2,1)} %get-tuple-element.93) | copy-start | bytes 129028

commit v4 on v3

--- a/solution.py
+++ b/solution.py
@@ -550,11 +550,12 @@
 
     third = R // 3
     NK = 32
-    local = []
+    AHEAD = 2
+    GAP = 2
+    LAG = AHEAD + (NZ + 1) * GAP
     for k in range(NK):
         cp = pltpu.make_async_copy(local_part(k), wref(k, f, 0, R), s_loc.at[k])
         cp.start()
-        local.append(cp)
 
     def vec_copy(step):
         return remote(
@@ -574,13 +575,21 @@
     def shard(zz, yy):
         return zz * 4 + yy * 2 + c
 
-    def z_copy(k, d):
-        ref = wref(k, f, third * x, 2 * third)
-        return remote(ref, ref, sz.at[k, d - 1], rz.at[k, d - 1], device(x, (z + d) % NZ, y, c))
+    def z_relay(k, way, dist):
+        up = way == 0
+        ref = wref(k, shard(z - dist if up else z + dist, y), third * x, 2 * third)
+        lands = dist + 1 if up else NZ - 1 - dist
+        return remote(
+            ref, ref, sz.at[k, way, dist], rz.at[k, lands - 1],
+            device(x, z + 1 if up else z - 1, y, c),
+        )
 
     def z_wait(k, d):
         ref = wref(k, shard((z + NZ - d) % NZ, y), third * x, 2 * third)
-        remote(ref, ref, sz.at[k, d - 1], rz.at[k, d - 1], device(x, (z + d) % NZ, y, c)).wait_recv()
+        remote(ref, ref, sz.at[k, 0, 0], rz.at[k, d - 1], device(x, z, 1 - y, c)).wait_recv()
+
+    def z_relay_when(way, dist):
+        return (z >= dist) & (z + 1 < NZ) if way == 0 else (z + dist < NZ) & (z >= 1)
 
     def y_copy(k, d):
         ref = wref(k, shard((z + NZ - d) % NZ, y), third * x, 2 * third)
@@ -607,40 +616,65 @@
         ref = wref(k, other, 0, R)
         remote(ref, ref, sc.at[k, 2 * d + e], rc.at[k, 2 * d + e], device(x, z, y, 1 - c)).wait_recv()
 
-    for k in range(NK):
-        local[k].wait()
-        for d in range(1, NZ):
-            z_copy(k, d).start()
+    def own_start(k):
+        ref = wref(k, f, 0, R)
+        pltpu.make_async_copy(ref, ref, s_loc.at[k]).wait()
+        for way in range(2):
+
+            @pl.when(z_relay_when(way, 0))
+            def _():
+                z_relay(k, way, 0).start()
+
         y_copy(k, 0).start()
         c_copy(k, 0, 0).start()
 
+    def z_stage(k, dist):
+        for way in range(2):
+            d = dist if way == 0 else NZ - dist
+
+            @pl.when(z >= dist if way == 0 else z + dist < NZ)
+            def _():
+                z_wait(k, d)
+
+                @pl.when((dist < NZ - 1) & (z + 1 < NZ if way == 0 else z >= 1))
+                def _():
+                    z_relay(k, way, dist).start()
+
+                y_copy(k, d).start()
+                x_copy(k, d, 0).start()
+
+    def y_stage(k):
+        def one(d):
+            y_wait(k, d)
+            x_copy(k, d, 1).start()
+
+        loop(NZ, one)
+
+    def x_stage(k):
+        def one(i):
+            d, e = (i + 1) % NZ, (i + 1) // NZ
+            x_wait(k, d, e)
+            c_copy(k, d, e).start()
+
+        loop(2 * NZ - 1, one)
+
+    def c_stage(k):
+        loop(2 * NZ, lambda i: c_wait(k, i % NZ, i // NZ))
+
     def gather_step(t):
-        @pl.when(t < NK)
-        def _():
-            for d in range(1, NZ):
-                z_wait(t, d)
-                y_copy(t, d).start()
-                x_copy(t, d, 0).start()
-
-        @pl.when((t >= 1) & (t < NK + 1))
-        def _():
-            for d in range(NZ):
-                y_wait(t - 1, d)
-                x_copy(t - 1, d, 1).start()
-
-        @pl.when((t >= 2) & (t < NK + 2))
-        def _():
-            for e in range(2):
-                for d in range(NZ):
-                    if d or e:
-                        x_wait(t - 2, d, e)
-                        c_copy(t - 2, d, e).start()
-
-        @pl.when(t >= 3)
-        def _():
-            for e in range(2):
-                for d in range(NZ):
-                    c_wait(t - 3, d, e)
+        def at(k, act):
+            @pl.when((k >= 0) & (k < NK))
+            def _():
+                act(k)
+
+        at(t, own_start)
+        loop(
+            NZ - 1,
+            lambda i: at(t - AHEAD - i * GAP, lambda k: z_stage(k, i + 1)),
+        )
+        at(t - AHEAD - (NZ - 1) * GAP, y_stage)
+        at(t - AHEAD - NZ * GAP, x_stage)
+        at(t - LAG, c_stage)
 
     def gather_steps(lo, hi):
         def step(t, carry):
@@ -648,6 +682,9 @@
             return carry
 
         lax.fori_loop(lo, hi, step, 0)
+
+    gather_steps(0, 2)
+    reached = [2]
 
     la, lva = g.la, g.lva
 
@@ -1180,45 +1217,53 @@
         total = total + dot(VEC[ff], pick)
     vecs[...] = total
 
-    reached = [0]
-
     def gather_to(t):
         if t > reached[0]:
             gather_steps(reached[0], t)
             reached[0] = t
 
     def gather_more(n):
-        gather_to(min(reached[0] + n, NK + 3))
+        gather_to(min(reached[0] + n, NK + LAG))
 
     def gather_sent(k):
-        for d in range(1, NZ):
-            z_copy(k, d).wait_send()
-        for d in range(NZ):
-            y_copy(k, d).wait_send()
-            for e in range(2):
-                c_copy(k, d, e).wait_send()
-                if d or e:
-                    x_copy(k, d, e).wait_send()
+        def hop(dist):
+            for way in range(2):
+
+                @pl.when(z_relay_when(way, dist))
+                def _():
+                    z_relay(k, way, dist).wait_send()
+
+        loop(NZ - 1, hop)
+        loop(NZ, lambda d: y_copy(k, d).wait_send())
+        loop(2 * NZ, lambda i: c_copy(k, i % NZ, i // NZ).wait_send())
+        loop(2 * NZ - 1, lambda i: x_copy(k, (i + 1) % NZ, (i + 1) // NZ).wait_send())
 
     for s in range(2):
-        base = 16 * s + 4
+        base = 16 * s + LAG + 1
         gather_to(base + 2)
         cross_project(s)
         gather_to(base + 3)
         attend(CQ, 0, s, 1 - s, p_refs[s], OC)
         if s == 1:
+            gather_more(1)
             z_collect(1, 0)
             spread_all(1, 0, "start")
+            gather_more(1)
         gather_to(base + 4)
         out_project(OC, 0, s)
         norm_forward(0, H1, s)
+        if s == 1:
+            gather_more(1)
         gather_to(base + 6)
         self_project(s)
+        if s == 1:
+            gather_more(1)
         gather_to(base + 7)
         attend(SQ, 0, s, s, p_refs[2 + s], OS)
         if s == 1:
             z_collect(0, 0)
             spread_all(0, 0, "start")
+            gather_more(1)
         gather_to(base + 8)
         out_project(OS, 1, s)
         norm_forward(1, H2, s)
@@ -1327,6 +1372,36 @@
     for n in range(2):
         for s in range(2):
             spread_all(n, s, "wait")
+
+
+def finish_kernel(g, *refs):
+    rows, (ga, gu, gd, vectors) = refs[:8], refs[8:12]
+    outs, (g_in, g_out, g_up, g_dn, g_gain, g_bias, g_gate) = refs[12:20], refs[20:]
+    for src, dst in zip(rows, outs):
+        dst[...] = src[...]
+
+    for s in range(2):
+
+        def unit(m):
+            g_in[s, m] = ga[s, m].astype(F32)
+
+        loop(6, unit)
+        for m in range(2):
+            g_out[s, m] = ga[s, 6 + m].astype(F32)
+        g_up[s] = gu[s].astype(F32)
+        g_dn[s] = gd[s].astype(F32)
+    row = lax.broadcasted_iota(jnp.int32, (g.d, g.rows), 0)
+    lane = lax.broadcasted_iota(jnp.int32, (g.d, g.rows), 1)
+    pick = jnp.where(row == lane + lax.axis_index("fsdp") * g.rows, 1.0, 0.0)
+    own = lax.dot_general(
+        vectors[...], pick, (((1,), (0,)), ((), ())),
+        precision=lax.Precision.HIGHEST, preferred_element_type=F32,
+    )
+    for s in range(2):
+        for i in range(3):
+            g_gain[s, i : i + 1] = own[3 * s + i : 3 * s + i + 1]
+            g_bias[s, i : i + 1] = own[6 + 3 * s + i : 7 + 3 * s + i]
+    g_gate[...] = own[12:14]
 
 
 def kernel_path(g, *args):
@@ -1380,7 +1455,7 @@
         dma(33),
         dma(g.fsdp - 1),
         dma(g.fsdp - 1),
-        dma(32, NZ - 1),
+        dma(32, 2, NZ - 1),
         dma(32, NZ - 1),
         dma(32, NZ),
         dma(32, NZ),
@@ -1412,18 +1487,23 @@
         ),
         name="layer",
     )(*lens, *rows, *cots, *weights, vec)
-    ga, gu, gd, vectors = results[8:12]
-    ga = ga.astype(F32)
-    own = lax.dynamic_slice(vectors, (0, lax.axis_index("fsdp") * R), (16, R))
-    return (
-        *results[:8],
-        ga[:, :6],
-        ga[:, 6:],
-        gu.astype(F32),
-        gd.astype(F32),
-        own[0:6].reshape(2, 3, R),
-        own[6:12].reshape(2, 3, R),
-        own[12:14],
+    grad_shapes = [
+        jax.ShapeDtypeStruct((2, 6, R, D), F32),
+        jax.ShapeDtypeStruct((2, 2, R, D), F32),
+        jax.ShapeDtypeStruct((2, R, FF), F32),
+        jax.ShapeDtypeStruct((2, 4 * R, D), F32),
+        jax.ShapeDtypeStruct((2, 3, R), F32),
+        jax.ShapeDtypeStruct((2, 3, R), F32),
+        jax.ShapeDtypeStruct((2, R), F32),
+    ]
+    return tuple(
+        pl.pallas_call(
+            partial(finish_kernel, g),
+            out_shape=row_shapes * 2 + grad_shapes,
+            in_specs=[in_vmem] * 12,
+            out_specs=[in_vmem] * 15,
+            name="finish",
+        )(*results[:12])
     )
 
 

time: 396 us -> 356 us (0.90)
  Pallas kernels: 376 us -> 347 us
  local copies, waits for them, and re-layouts: 13.3 us -> 3.91 us
    pallas_call x1, Pallas kernels: 376 us -> 343 us  [kernel_path(): pl.pallas_call(partial(layer_kernel, g), out_shape=out_shape, in_specs=[i...]
    unnamed x34 -> x2, local copies, waits for them, and re-layouts: 7.59 us -> 1.37 us
    slice x4 -> x0, local copies, waits for them, and re-layouts: 5.65 us -> none  [the longest x1 2.6 us: kernel_path(): ga[:, :6]]
    pallas_call x0 -> x1, Pallas kernels: none -> 4.48 us  [kernel_path(): pl.pallas_call(partial(finish_kernel, g), out_shape=row_shapes * 2 + grad...]
where the time goes in v4:
time: 356 us
  Pallas kernels  347 us (97%)
  local copies, waits for them, and re-layouts  3.91 us (1%)
    pallas_call x1, Pallas kernels, kernel_path(): pl.pallas_call(partial(layer_kernel, g), out_shape=out_shape, in_specs=[i...  343 us

profile of v4, /device:TPU:31, one launch (start us, length us, event | category | flops | bytes accessed | tf_op | source)
XLA Modules:
  0.0 355.6 jit_solution(5264709341056472772)
XLA Ops:
  3.2 0.7 copy.38
  3.9 0.7 copy.39
  4.6 1.3 fusion.8.refs_16_
  5.9 342.7 %layer.1 = (bf16[1,48,768]{2,1,0:T(8,128)(2,1)}, bf16[1,20,768]{2,1,0:T(8,128)(2,1)}, bf16[1,56,768]{2,1,0:T(8,128)(2,1)}, bf16[1,28,768]{2,1,0:T(8,128)(2,1)}, ...) custom-call(s32[1]{0:T(128)S(6)} %copy.42.refs_0_, ...), custom_call_target="tpu_custom_call" | custom-call | tf_op jit(solution)/shard_map/layer/pallas_call | solution.py:1479
  348.6 4.5 %finish.1 = (bf16[1,48,768]{2,1,0:T(8,128)(2,1)}, bf16[1,20,768]{2,1,0:T(8,128)(2,1)}, bf16[1,56,768]{2,1,0:T(8,128)(2,1)}, bf16[1,28,768]{2,1,0:T(8,128)(2,1)},...) custom-call(bf16[1,48,768]{2,1,0:T(8,128)(2,1)} %get-tuple-element.2, ...), custom_call_target="tpu_custom_call" | custom-call | tf_op jit(solution)/shard_map/finish/pallas_call | solution.py:1500
  353.1 1.3 copy.40
  354.3 1.3 copy.41
  (2 shorter events, 0.0 us)

commit v5 on v4

--- a/solution.py
+++ b/solution.py
@@ -908,14 +908,15 @@
 
         loop(NT, tile)
 
-    def ffn_down_back(s):
+    def ffn_down_back(s, q):
         own = span[s]
 
-        def tile(j):
-            da = dot_rt(S[DF, own], wrows(s, 12 + j // NT, j % NT))
+        def tile(i):
+            j = q * NT + i
+            da = dot_rt(S[DF, own], wrows(s, 12 + q, i))
             DU[own, cols(j, 256)] = (GP[own, cols(j, 256)] * da).astype(BF)
 
-        loop(4 * NT, tile)
+        loop(NT, tile)
 
     def ffn_up_back(s):
         own = span[s]
@@ -1281,8 +1282,8 @@
         for r in range(4, 8):
             send_ffn_right(r, s)
         gather_more(1)
-        ffn_down_back(s)
         for r in range(4):
+            ffn_down_back(s, r)
             send_ffn_right(r, s)
         for r in range(8):
             send_left(r, s)
@@ -1292,12 +1293,12 @@
         send_right(7, s)
         gather_more(1)
         out_back(DS, 1, s)
+        lax.fori_loop(16 * s, 16 * s + 16, lambda k, carry: (gather_sent(k), carry)[1], 0)
+        ffn_share(s)
         attend_back(SQ, 0, s, s, p_refs[2 + s], DQS, DKS, DVS)
         for r in (4, 5, 6):
             send_right(r, s)
         gather_more(1)
-        lax.fori_loop(16 * s, 16 * s + 16, lambda k, carry: (gather_sent(k), carry)[1], 0)
-        ffn_share(s)
         gather_more(1)
         self_back(s)
         norm_backward(0, DC, s)

time: 356 us -> 351 us (0.986); the launches traced: 356 us -> 346 us
  Pallas kernels: 347 us -> 338 us
    pallas_call x1, Pallas kernels: 343 us -> 333 us  [kernel_path(): pl.pallas_call(partial(layer_kernel, g), out_shape=out_shape, in_specs=[i...]
where the time goes in v5:
time: 351 us; the launch traced here: 346 us
  Pallas kernels  338 us (96%)
  local copies, waits for them, and re-layouts  3.91 us (1%)
    pallas_call x1, Pallas kernels, kernel_path(): pl.pallas_call(partial(layer_kernel, g), out_shape=out_shape, in_specs=[i...  333 us

profile of v5, /device:TPU:31, one launch (start us, length us, event | category | flops | bytes accessed | tf_op | source)
XLA Modules:
  0.0 345.9 jit_solution(6670803644837756653)
XLA Ops:
  3.2 0.7 copy.38
  3.9 0.7 copy.39
  4.6 1.3 fusion.8.refs_16_
  5.9 333.1 %layer.1 = (bf16[1,48,768]{2,1,0:T(8,128)(2,1)}, bf16[1,20,768]{2,1,0:T(8,128)(2,1)}, bf16[1,56,768]{2,1,0:T(8,128)(2,1)}, bf16[1,28,768]{2,1,0:T(8,128)(2,1)}, ...) custom-call(s32[1]{0:T(128)S(6)} %copy.42.refs_0_, ...), custom_call_target="tpu_custom_call" | custom-call | tf_op jit(solution)/shard_map/layer/pallas_call | solution.py:1480
  339.0 4.5 %finish.1 = (bf16[1,48,768]{2,1,0:T(8,128)(2,1)}, bf16[1,20,768]{2,1,0:T(8,128)(2,1)}, bf16[1,56,768]{2,1,0:T(8,128)(2,1)}, bf16[1,28,768]{2,1,0:T(8,128)(2,1)},...) custom-call(bf16[1,48,768]{2,1,0:T(8,128)(2,1)} %get-tuple-element.2, ...), custom_call_target="tpu_custom_call" | custom-call | tf_op jit(solution)/shard_map/finish/pallas_call | solution.py:1501
  343.4 1.3 copy.40
  344.7 1.3 copy.41
  (2 shorter events, 0.0 us)
